TPU v7x, 32 devices: a whole 2x2x4 slice. The times are simulated.
32 devices in a mesh: row: 4 (over z), col: 4 (over y, core), occ: 2 (over x).
Axes of the slice: x: 2, y: 2, z: 4, core: 2. Of those that a mesh axis runs over, the one named last changes fastest.
Arguments:
- doubles: float32 [4, 2048, 4, 2048], P(None, 'row', 'occ', 'col'), may hold values from -6 to 6
- cycle: float32 [4, 2048, 4, 2048], P('occ', 'row', None, 'col'), may hold values from -0.0625 to 0.0625
- occ_energy: float32 [4], replicated, may hold values from -3 to -0.5
- virt_energy: float32 [2048], replicated, may hold values from 0.5 to 3
- orbital_irrep: int32 [2052], replicated, may hold values from 0 to 3
Outputs:
- update: float32 [4, 2048, 4, 2048], P(None, 'row', 'occ', 'col')
Inputs may be any that keep to these rules, and one draw needn't show every extreme that they name: `orbital_irrep`: C2v irrep labels; the product of two irreps is the bitwise xor of their labels.
All inputs are finite; a program needn't handle non-finite values.
Results may differ from a plain program's by a relative error of at most 0.00007.
Values sent between devices are 32-bit elements; how exact they have to be, the bound alone decides.
No kernel may reach another device: no remote copies, remote signals or barrier semaphores. Data moves between devices by JAX's collectives and lax.ppermute only.
A program may use at most 192 MiB of HBM per device.

v0:
```python
import jax
import jax.numpy as jnp
from jax import lax
from jax.sharding import PartitionSpec as P


def contract(left_part, right_part):
    n_i, tile_a, k_part, c_part = left_part.shape
    n_j, tile_b = (right_part.shape[2], right_part.shape[3])
    product = jnp.dot(
        left_part.reshape(n_i * tile_a, k_part * c_part),
        right_part.reshape(k_part * c_part, n_j * tile_b),
        precision=lax.Precision.HIGHEST,
        preferred_element_type=jnp.float32,
    )
    return product


def shards(doubles, cycle, occ_energy, virt_energy, orbital_irrep):
    n_i, tile_a, k_half, tile_c = doubles.shape
    n_j, tile_b = (cycle.shape[2], cycle.shape[3])
    half_occ = n_j // lax.axis_size("occ")
    occ_irrep = orbital_irrep[:n_j]
    virt_irrep = orbital_irrep[n_j:]
    doubles_full = lax.all_gather(doubles, "col", axis=3, tiled=True)
    partial_flat = contract(doubles_full, lax.all_gather(cycle, "row", axis=1, tiled=True))
    partial_value = partial_flat.reshape(n_i, tile_a, n_j, tile_b)
    occ_pos = lax.axis_index("occ")
    own_sum = lax.psum_scatter(partial_value, "occ", scatter_dimension=2, tiled=True)
    held = lax.all_to_all(own_sum, "occ", split_axis=0, concat_axis=2, tiled=True)
    row_pos = lax.axis_index("row")
    col_pos = lax.axis_index("col")
    held = lax.all_to_all(
        lax.all_to_all(held, "row", split_axis=1, concat_axis=1, tiled=True),
        "col",
        split_axis=1,
        concat_axis=1,
        tiled=True,
    )
    held = lax.all_to_all(held, "row", split_axis=1, concat_axis=1, tiled=True)
    paired = own_sum + jnp.transpose(held, (2, 3, 0, 1))
    energy_a = lax.dynamic_slice_in_dim(virt_energy, row_pos * tile_a, tile_a, 0)
    energy_b = lax.dynamic_slice_in_dim(virt_energy, col_pos * tile_b, tile_b, 0)
    energy_j = lax.dynamic_slice_in_dim(occ_energy, occ_pos * half_occ, half_occ, 0)
    irrep_a = lax.dynamic_slice_in_dim(virt_irrep, row_pos * tile_a, tile_a, 0)
    irrep_b = lax.dynamic_slice_in_dim(virt_irrep, col_pos * tile_b, tile_b, 0)
    irrep_j = lax.dynamic_slice_in_dim(occ_irrep, occ_pos * half_occ, half_occ, 0)
    denom = (
        energy_a[None, :, None, None]
        + energy_b[None, None, None, :]
        - occ_energy[:, None, None, None]
        - energy_j[None, None, :, None]
    )
    sector = jnp.bitwise_xor(
        jnp.bitwise_xor(occ_irrep[:, None, None, None], irrep_a[None, :, None, None]),
        jnp.bitwise_xor(irrep_j[None, None, :, None], irrep_b[None, None, None, :]),
    )
    return jnp.where(sector == 0, paired / denom, jnp.zeros_like(paired))


def solution(mesh):
    return jax.shard_map(
        shards,
        mesh=mesh,
        in_specs=(P(None, "row", "occ", "col"), P("occ", "row", None, "col"), P(), P(), P()),
        out_specs=P(None, "row", "occ", "col"),
        check_vma=False,
    )
```

profile of v0, /device:TPU:0, one launch (start us, length us, event | category | flops | bytes accessed | tf_op | source)
XLA Modules:
  0.0 2046.4 jit_solution(14824591665897296054)
XLA Ops:
  6.5 0.0 all-gather.5.cloned.1.call-start
  6.5 0.7 all-gather.5.cloned.1.call-update
  7.3 0.0 all-gather.3.cloned.1.call-start
  7.3 0.7 all-gather.3.cloned.1.call-update
  8.0 0.0 all-reduce.3.cloned.1.call-start
  8.1 565.0 %all-gather.5.cloned.1.call-done = f32[2,2048,4,512]{3,2,1,0:T(4,128)} async-done(((f32[2,512,4,512]{3,2,1,0:T(4,128)}), f32[2,2048,4,512]{3,2,1,0:T(4,128)}) %all-gather.5.cloned.1.call-update) | async-done | bytes 33554448 | tf_op jit(solution)/shard_map/all_gather | solution.py:26
  573.1 31.1 %copy.16 = f32[512,8,4,512]{3,1,2,0:T(8,128)} copy(f32[512,8,4,512]{3,2,1,0:T(4,128)} %bitcast.32) | data formatting | bytes 67108864
  604.2 31.4 %copy.9 = f32[4096,2048]{0,1:T(8,128)} copy(f32[4096,2048]{1,0:T(8,128)} %bitcast.31) | data formatting | bytes 67108864 | tf_op jit(solution)/shard_map/reshape | solution.py:12
  635.6 143.3 %all-gather.3.cloned.1.call-done = f32[4,512,2,2048]{3,2,1,0:T(2,128)} async-done(((f32[4,512,2,512]{3,2,1,0:T(2,128)}), f32[4,512,2,2048]{3,2,1,0:T(2,128)}) %all-gather.3.cloned.1.call-update) | async-done | bytes 33554448 | tf_op jit(solution)/shard_map/all_gather | solution.py:25
  778.9 42.8 %reshape.112 = f32[4,512,4096,1]{2,1,0,3:T(8,128)} reshape(f32[4,512,2,2048]{3,2,1,0:T(2,128)} %all-gather.3.cloned.1.call-done) | data formatting | bytes 67108864 | tf_op jit(solution)/shard_map/dot_general | solution.py:10
  821.7 221.8 %fusion = f32[4,512,4,512]{3,1,2,0:T(8,128)} fusion(f32[4,512,4096,1]{2,1,0,3:T(8,128)} %bitcast.33, f32[4,512,4096,1]{2,1,0,3:T(8,128)} %reshape.112), kind=kOutput, calls=%fused_computation | convolution fusion | flops 206158430208 | bytes 83886080 | tf_op jit(solution)/shard_map/dot_general | solution.py:10
  1043.4 0.0 copy-start.3
  1043.4 0.0 all-reduce.3.cloned.1.call-update
  1043.5 0.6 copy-done.3
  1044.1 0.6 dynamic-slice
  1045.3 376.3 %all-reduce.3.cloned.1.call-done = f32[4,512,4,512]{3,1,2,0:T(8,128)} async-done(((f32[4,512,4,512]{3,1,2,0:T(8,128)}), f32[4,512,4,512]{3,1,2,0:T(8,128)}) %all-reduce.3.cloned.1.call-update) | async-done | bytes 16777232
  1421.6 4.4 constant_dynamic-slice_fusion
  1426.0 95.6 %all_to_all.33 = f32[4,512,2,512]{3,1,2,0:T(8,128)S(1)} all-to-all(f32[4,512,2,512]{3,1,2,0:T(8,128)S(1)} %constant_dynamic-slice_fusion), channel_id=1, replica_groups=mesh['row'=4,'col'=4,'occ'=2] {'occ'}, dimensions={0} | all-to-all | bytes 16777216 | tf_op jit(solution)/shard_map/all_to_all | solution.py:30
  1521.7 7.7 copy.10
  1529.4 186.5 %all_to_all.34 = f32[2,512,4,512]{3,0,2,1:T(2,128)S(1)} all-to-all(f32[2,512,4,512]{3,0,2,1:T(2,128)S(1)} %bitcast.35), channel_id=1, replica_groups=mesh['row'=4,'col'=4,'occ'=2] {'row'}, dimensions={1} | all-to-all | bytes 16777216 | tf_op jit(solution)/shard_map/all_to_all | solution.py:34
  1716.0 96.9 %all_to_all.35 = f32[2,512,4,512]{3,0,2,1:T(2,128)} all-to-all(f32[2,512,4,512]{3,0,2,1:T(2,128)S(1)} %all_to_all.34), channel_id=1, replica_groups=mesh['row'=4,'col'=4,'occ'=2] {'col'}, dimensions={1} | all-to-all | bytes 16777216 | tf_op jit(solution)/shard_map/all_to_all | solution.py:33
  1812.9 0.0 copy-start
  1812.9 0.0 copy-start.2
  1812.9 0.0 copy-start.1
  1812.9 5.8 all-to-all-start.3
  1818.7 0.0 copy-done
  1818.7 0.1 slice.7
  1818.7 0.0 copy-done.2
  1818.7 0.1 dynamic_slice.23
  1818.8 0.1 dynamic_slice.19
  1818.9 0.0 copy-done.1
  1818.9 0.1 fusion.5
  1819.0 0.1 fusion.4
  1819.1 0.1 broadcast_xor_fusion.1
  1819.1 0.1 broadcast_xor_fusion
  1819.2 0.1 broadcast_add_fusion
  1819.3 2.7 broadcast_subtract_fusion
  1822.0 179.6 %all-to-all-done.3 = f32[2,512,4,512]{3,0,2,1:T(2,128)} async-done(((f32[2,512,4,512]{3,0,2,1:T(2,128)}), f32[2,512,4,512]{3,0,2,1:T(2,128)}, u32[]{:S(2)}, u32[]{:S(2)}) %all-to-all-start.3) | async-done | bytes 8388640 | tf_op jit(solution)/shard_map/all_to_all | solution.py:40
  2001.6 13.1 copy.11
  2014.8 8.1 fusion.3
  2022.9 17.0 copy.12
  (1 shorter events, 0.0 us)
Async XLA Ops:
  6.5 566.5 %all-gather.5.cloned.1.call-start = ((), (), s32[]{:S(2)}) async-start(), calls=%async_computation.5 | async-start | bytes 41943040 | tf_op jit(solution)/shard_map/all_gather | solution.py:26
  7.3 771.6 %all-gather.3.cloned.1.call-start = ((), (), s32[]{:S(2)}) async-start(), calls=%async_computation.4 | async-start | bytes 41943040 | tf_op jit(solution)/shard_map/all_gather | solution.py:25
  8.0 1413.6 %all-reduce.3.cloned.1.call-start = ((), (), s32[]{:S(2)}) async-start(), calls=%async_computation.6 | async-start | bytes 33554432
  1043.4 0.7 copy-start.3
  1812.9 5.8 copy-start
  1812.9 5.9 copy-start.2
  1812.9 6.0 copy-start.1
  1812.9 188.8 %all-to-all-start.3 = ((f32[2,512,4,512]{3,0,2,1:T(2,128)}), f32[2,512,4,512]{3,0,2,1:T(2,128)}, u32[]{:S(2)}, u32[]{:S(2)}) async-start(f32[2,512,4,512]{3,0,2,1:T(2,128)} %all_to_all.35), calls=%async_computation.3 | async-start | bytes 16777216 | tf_op jit(solution)/shard_map/all_to_all | solution.py:40
Sparse Core Ops, SparseCore 0:
  8.9 564.0 all-gather.4
  574.6 204.1 all-gather.2
  1043.6 377.9 all-reduce.2
where the time goes:
time: 2050 us
  waiting for transfers between devices  1270 us (62%)
  blocking collectives  379 us (18%)
  matrix products  222 us (11%)
  local copies, waits for them, and re-layouts  149 us (7%)
    all_gather x1, waiting for transfers between devices, shards(): lax.all_gather(cycle, 'row', axis=1, tiled=True)  565 us
    unnamed x4, waiting for transfers between devices  378 us
    dot_general x1, matrix products, contract(): jnp.dot(left_part.reshape(n_i * tile_a, k_part * c_part), right_part.resh...  222 us
    all_to_all x1, blocking collectives, shards(): lax.all_to_all(held, 'row', split_axis=1, concat_axis=1, tiled=True)  187 us
    all_to_all x1, waiting for transfers between devices, shards(): held = lax.all_to_all(held, 'row', split_axis=1, concat_axis=1, tiled=True)  180 us
    all_gather x1, waiting for transfers between devices, shards(): doubles_full = lax.all_gather(doubles, 'col', axis=3, tiled=True)  143 us
    all_to_all x1, blocking collectives, shards(): lax.all_to_all(lax.all_to_all(held, 'row', split_axis=1, concat_axis=1, t...  96.9 us
    all_to_all x1, blocking collectives, shards(): lax.all_to_all(own_sum, 'occ', split_axis=0, concat_axis=2, tiled=True)  95.6 us
  transfers between devices with their start and end apart: 4, of which 4 were waited for; matrix products, arithmetic and copies ran while one was open for 3% of the time, Pallas kernels for 0%

commit v1 on v0

v1 whole, which is shorter than its diff:
```python
import functools

import jax
import jax.numpy as jnp
from jax import lax
from jax.experimental import pallas as pl
from jax.experimental.pallas import tpu as pltpu
from jax.sharding import PartitionSpec as P

N_IRREPS = 4
VMEM_LIMIT = 56 * 1024 * 1024


def split(x):
    high = x.astype(jnp.bfloat16)
    low = (x - high.astype(jnp.float32)).astype(jnp.bfloat16)
    return high, low


def dot(a, b, contract=((1,), (0,))):
    return lax.dot_general(a, b, (contract, ((), ())), preferred_element_type=jnp.float32)


def sort_body(place_ref, rows_ref, out_ref):
    tile_a, depth = rows_ref.shape[1:]
    chunks, n_piece, _, sub, _ = out_ref.shape[1:]
    places = lax.broadcasted_iota(jnp.int32, (tile_a, tile_a), 0)
    order = (place_ref[...] == places).astype(jnp.float32).astype(jnp.bfloat16)
    high, low = split(rows_ref[0])
    value = dot(order, high) + dot(order, low)
    out_ref[0, :, :, 0] = value.reshape(chunks, n_piece, sub, depth)


def sort_rows(doubles, place, n_occ, chunks, n):
    n_i, tile_a, k_half, tile_c = doubles.shape
    half, sub = n_i // n_occ, tile_a // (chunks * n)
    shape = (half, chunks, n, n_occ, sub, k_half * tile_c)
    return pl.pallas_call(
        sort_body,
        out_shape=jax.ShapeDtypeStruct(shape, jnp.float32),
        grid=(half, n_occ),
        in_specs=[
            pl.BlockSpec((1, tile_a), lambda m, o: (0, 0)),
            pl.BlockSpec((1, tile_a, k_half * tile_c), lambda m, o: (o * half + m, 0, 0)),
        ],
        out_specs=pl.BlockSpec((1, chunks, n, 1, sub, k_half * tile_c), lambda m, o: (m, 0, 0, o, 0, 0)),
        compiler_params=pltpu.CompilerParams(vmem_limit_bytes=VMEM_LIMIT),
        cost_estimate=pl.CostEstimate(
            flops=4 * doubles.size * tile_a, bytes_accessed=8 * doubles.size, transcendentals=0
        ),
    )(place, doubles.reshape(n_i, tile_a, k_half * tile_c))


def compact_body(cap, key_ref, right_ref, high_ref, low_ref, select_ref, both_ref):
    n_j, tile_b = select_ref.shape[:2]
    width = N_IRREPS * cap

    @pl.when(pl.program_id(0) == 0)
    def _():
        for j in range(n_j):
            slots = lax.broadcasted_iota(jnp.int32, (tile_b, width), 1)
            select_ref[j] = (key_ref[j] == slots).astype(jnp.float32).astype(jnp.bfloat16)

    rows = right_ref.shape[0]
    for j in range(n_j):
        high, low = split(right_ref[:, j * tile_b : (j + 1) * tile_b])
        both_ref[j, :rows] = high
        both_ref[j, rows:] = low

    @pl.loop(0, N_IRREPS)
    def _(q):
        span = pl.ds(pl.multiple_of(q * cap, 128), cap)
        total = dot(both_ref[0], select_ref[0, :, span])
        for j in range(1, n_j):
            total += dot(both_ref[j], select_ref[j, :, span])
        high_ref[:, span] = total[:rows].astype(jnp.bfloat16)
        low_ref[:, span] = total[rows:].astype(jnp.bfloat16)


def compact(right, key, cap):
    k_half, tile_c, n_j, tile_b = right.shape
    step = min(tile_c, 256)
    width = N_IRREPS * cap
    out = jax.ShapeDtypeStruct((k_half * tile_c, width), jnp.bfloat16)
    return pl.pallas_call(
        functools.partial(compact_body, cap),
        out_shape=(out, out),
        grid=(k_half * tile_c // step,),
        in_specs=[
            pl.BlockSpec((n_j, tile_b, 1), lambda s: (0, 0, 0)),
            pl.BlockSpec((step, n_j * tile_b), lambda s: (s, 0)),
        ],
        out_specs=[pl.BlockSpec((step, width), lambda s: (s, 0))] * 2,
        scratch_shapes=[
            pltpu.VMEM((n_j, tile_b, width), jnp.bfloat16),
            pltpu.VMEM((n_j, 2 * step, tile_b), jnp.bfloat16),
        ],
        compiler_params=pltpu.CompilerParams(vmem_limit_bytes=VMEM_LIMIT),
        cost_estimate=pl.CostEstimate(
            flops=4 * k_half * tile_c * n_j * tile_b * width, bytes_accessed=4 * right.size, transcendentals=0
        ),
    )(key, right.reshape(k_half * tile_c, n_j * tile_b))


def product_body(cap, scalar_ref, irrep_ref, near_ref, far_ref, high_ref, low_ref, out_ref, *scratch):
    left_high_ref, left_low_ref = scratch
    n_row, _, sub, depth = near_ref.shape[1:]
    row_pos, col_pos, row_i = scalar_ref[1], scalar_ref[2], scalar_ref[3]
    for at, ref in enumerate((near_ref, far_ref)):
        left_high_ref[at], left_low_ref[at] = split(ref[0, :, 0].reshape(n_row * sub, depth))
    out_ref[...] = jnp.zeros_like(out_ref)

    @pl.loop(0, 2 * N_IRREPS)
    def _(step):
        at, irrep = step // N_IRREPS, step % N_IRREPS
        place = jnp.bitwise_xor(col_pos, at) % 2
        piece = jnp.bitwise_xor(col_pos, 2 * pl.program_id(0) + at)

        @pl.when(scalar_ref[4 + piece * N_IRREPS + irrep] > 0)
        def _():
            span = pl.ds(pl.multiple_of(jnp.bitwise_xor(irrep, row_i) * cap, 128), cap)
            right_high = high_ref[:, span]
            left_high = left_high_ref[at]
            value = dot(left_low_ref[at], right_high) + dot(left_high, low_ref[:, span])
            value += dot(left_high, right_high)
            for t in range(n_row):
                r = jnp.bitwise_xor(row_pos, t)
                part = value[t * sub : (t + 1) * sub]
                out_ref[r, place] = jnp.where(irrep_ref[r, place] == irrep, part, out_ref[r, place])


def product(scalars, row_irrep, near, far, right_high, right_low, cap):
    n_pair, n_row, _, sub, depth = near.shape
    width = right_high.shape[1]
    pair = lambda v, scalars: (0, jnp.bitwise_xor(scalars[2] // 2, v), 0, 0)
    left = pl.BlockSpec((1, n_row, 1, sub, depth), lambda v, scalars: (v, 0, scalars[0], 0, 0))
    right = pl.BlockSpec((depth, width), lambda v, scalars: (0, 0), pipeline_mode=pl.Buffered(1))
    spec = pltpu.PrefetchScalarGridSpec(
        num_scalar_prefetch=1,
        grid=(n_pair,),
        in_specs=[pl.BlockSpec((n_row, 2, sub, 1), pair), left, left, right, right],
        out_specs=pl.BlockSpec((n_row, 2, sub, cap), pair),
        scratch_shapes=[pltpu.VMEM((2, n_row * sub, depth), jnp.bfloat16)] * 2,
    )
    rows = 2 * n_pair * n_row * sub
    return pl.pallas_call(
        functools.partial(product_body, cap),
        out_shape=jax.ShapeDtypeStruct((n_row, 2 * n_pair, sub, cap), jnp.float32),
        grid_spec=spec,
        compiler_params=pltpu.CompilerParams(vmem_limit_bytes=VMEM_LIMIT),
        cost_estimate=pl.CostEstimate(
            flops=3 * rows * depth * width, bytes_accessed=4 * rows * depth + 4 * depth * width, transcendentals=0
        ),
    )(scalars, row_irrep, near, far, right_high, right_low)


def finish_body(
    cap, occ_pos_ref, key_c_ref, slot_r_ref, irrep_i_ref, irrep_a_ref, place_a_ref, place_b_ref, irrep_jb_ref,
    energy_a_ref, energy_b_ref, energy_ij_ref, own_ref, swapped_ref, turned_ref, *refs,
):
    base_ref = refs[0] if len(refs) == 5 else None
    out_ref, expand_ref, turned_high_ref, turned_low_ref = refs[-4:]
    i = pl.program_id(0)
    half, tile_b = key_c_ref.shape
    tile_a = own_ref.shape[1]
    rows = out_ref.shape[1]

    def one_hot(column, length):
        hit = column == lax.broadcasted_iota(jnp.int32, (column.shape[0], length), 1)
        return hit.astype(jnp.float32).astype(jnp.bfloat16)

    @pl.when((i == 0) & (pl.program_id(1) == 0))
    def _():
        unsort = one_hot(place_b_ref[...], tile_b)
        slots = lax.broadcasted_iota(jnp.int32, (cap, tile_b), 0)
        for j in range(half):
            span = pl.ds(j * tile_b, tile_b)
            hit = key_c_ref[pl.ds(j, 1), :] == slots
            expand_ref[:, span] = hit.astype(jnp.float32).astype(jnp.bfloat16)
            high, low = split(turned_ref[j])
            turned_high_ref[span, :] = dot(unsort, high).astype(jnp.bfloat16)
            turned_low_ref[span, :] = dot(unsort, low).astype(jnp.bfloat16)

    mine = i // half == occ_pos_ref[0]
    unsort = one_hot(place_a_ref[...], tile_a)
    high, low = split(jnp.where(mine, own_ref[0], swapped_ref[0]))
    high, low = dot(unsort, high).astype(jnp.bfloat16), dot(unsort, low).astype(jnp.bfloat16)
    direct = dot(high, expand_ref[...]) + dot(low, expand_ref[...])
    pick = one_hot(slot_r_ref[0], cap)
    across = ((1,), (1,))
    turned = dot(pick, turned_high_ref[...], across) + dot(pick, turned_low_ref[...], across)
    paired = direct + turned
    row_class = jnp.bitwise_xor(irrep_a_ref[...], irrep_i_ref[i])
    for j in range(half):
        piece = paired[:, j * tile_b : (j + 1) * tile_b]
        denom = energy_a_ref[...] + energy_b_ref[...] - energy_ij_ref[i] - energy_ij_ref[2 * half + j]
        value = jnp.where(row_class == irrep_jb_ref[pl.ds(j, 1), :], piece / denom, jnp.zeros_like(piece))
        if base_ref is not None:
            value = value + base_ref[0, :, j, :]
        out_ref[0, :, j, :] = value


def finish(tables, own, swapped, turned, base, cap, shape):
    n_i, tile_a, half, tile_b = shape
    rows = min(tile_a, 256)
    block = pl.BlockSpec((1, rows, half, tile_b), lambda i, s: (i, s, 0, 0))
    part = pl.BlockSpec((1, tile_a, cap), lambda i, s: (i % half, 0, 0))
    smem = pl.BlockSpec(memory_space=pltpu.SMEM)
    whole = lambda x: pl.BlockSpec(x.shape, lambda i, s: (0,) * x.ndim)
    column = pl.BlockSpec((rows, 1), lambda i, s: (s, 0))
    occ_pos, key_c, slot_r, irrep_i, irrep_a, place_a, place_b, irrep_jb, energy_a, energy_b, energy_ij = tables
    args = list(tables) + [own, swapped, turned]
    specs = [
        smem, whole(key_c), pl.BlockSpec((1, rows, 1), lambda i, s: (i, s, 0)), smem, column, column, whole(place_b),
        whole(irrep_jb), column, whole(energy_b), smem, part, part, whole(turned),
    ]
    aliases = {}
    if base is not None:
        aliases = {len(args): 0}
        args.append(base)
        specs.append(block)
    return pl.pallas_call(
        functools.partial(finish_body, cap),
        out_shape=jax.ShapeDtypeStruct(shape, jnp.float32),
        grid=(n_i, tile_a // rows),
        in_specs=specs,
        out_specs=block,
        scratch_shapes=[
            pltpu.VMEM((cap, half * tile_b), jnp.bfloat16),
            pltpu.VMEM((half * tile_b, cap), jnp.bfloat16),
            pltpu.VMEM((half * tile_b, cap), jnp.bfloat16),
        ],
        input_output_aliases=aliases,
        compiler_params=pltpu.CompilerParams(vmem_limit_bytes=VMEM_LIMIT),
        cost_estimate=pl.CostEstimate(
            flops=8 * n_i * tile_a * cap * half * tile_b, bytes_accessed=4 * n_i * tile_a * (half * tile_b + cap),
            transcendentals=0,
        ),
    )(*args)


def after(x, *others):
    return lax.optimization_barrier((x,) + others)


def flipped(x, axis, n, bits):
    return lax.ppermute(x, axis, [(d, d ^ bits) for d in range(n)])


def exchange(pick, axis, n):
    return jnp.stack([pick(0)] + [flipped(pick(t), axis, n, t) for t in range(1, n)])


def turn(x, n):
    for axis in ("col", "row", "col"):
        x = lax.all_to_all(x, axis, split_axis=0, concat_axis=0, tiled=True)
    return x


def shards(doubles, cycle, occ_energy, virt_energy, orbital_irrep):
    n_i, tile_a, k_half, tile_c = doubles.shape
    n_j, tile_b = cycle.shape[2:]
    n, n_occ = lax.axis_size("row"), lax.axis_size("occ")
    half = n_j // n_occ
    columns = n_j * tile_b
    cap = min(columns, -(-columns * 5 // (N_IRREPS * 4 * 128)) * 128)
    chunks = 2 if tile_a % (16 * n) == 0 else 1
    sub = tile_a // (chunks * n)
    row_pos, col_pos, occ_pos = lax.axis_index("row"), lax.axis_index("col"), lax.axis_index("occ")
    occ_irrep, virt_irrep = orbital_irrep[:n_j], orbital_irrep[n_j:]

    blocks = virt_irrep.reshape(n, tile_b)
    kinds = jnp.arange(N_IRREPS, dtype=jnp.int32)
    counts = jnp.sum((blocks[:, None, :] == kinds[:, None]).astype(jnp.int32), axis=2)
    sizes = sum(counts[:, jnp.bitwise_xor(kinds, occ_irrep[j])] for j in range(n_j))
    rounds = (jnp.max(sizes) + cap - 1) // cap

    starts = jnp.cumsum(counts, axis=1) - counts

    def places(block_pos):
        irrep = lax.dynamic_index_in_dim(blocks, block_pos, 0, keepdims=False)
        count = lax.dynamic_index_in_dim(counts, block_pos, 0, keepdims=False)
        start = lax.dynamic_index_in_dim(starts, block_pos, 0, keepdims=False)
        order = jnp.arange(tile_b, dtype=jnp.int32)
        earlier = (irrep[:, None] == irrep[None, :]) & (order[:, None] < order[None, :])
        rank = jnp.sum(earlier.astype(jnp.int32), axis=0)
        look_up = lambda table, index: sum(jnp.where(index == g, table[g], 0) for g in range(N_IRREPS))
        slots = []
        for j in range(n_j):
            before = jnp.zeros((tile_b,), jnp.int32)
            for other in range(j):
                before += look_up(count, jnp.bitwise_xor(irrep, jnp.bitwise_xor(occ_irrep[j], occ_irrep[other])))
            slots.append(before + rank)
        return jnp.stack(slots), jnp.bitwise_xor(irrep[None, :], occ_irrep[:, None]), look_up(start, irrep) + rank

    slot_c, class_c, place_c = places(col_pos)
    slot_r, _, place_r = places(row_pos)

    order = jnp.arange(tile_a, dtype=jnp.int32)
    row_irrep = sum((order[None, :] >= starts[:, g, None]).astype(jnp.int32) for g in range(1, N_IRREPS))
    row_irrep = row_irrep.reshape(n, chunks, n, sub, 1)
    has = jnp.max((row_irrep == kinds).astype(jnp.int32), axis=(0, 3)).reshape(chunks, n * N_IRREPS)

    own_a = lambda x: lax.dynamic_slice_in_dim(x, row_pos * tile_a, tile_a, 0)
    own_b = lambda x: lax.dynamic_slice_in_dim(x, col_pos * tile_b, tile_b, 0)
    own_j = lambda x: lax.dynamic_slice_in_dim(x, occ_pos * half, half, 0)
    fixed = (
        occ_irrep, own_a(virt_irrep)[:, None], place_r[:, None], place_c[:, None], own_j(class_c),
        own_a(virt_energy)[:, None], own_b(virt_energy)[None, :], jnp.concatenate([occ_energy, own_j(occ_energy)]),
    )

    def one_round(doubles, cycle, number, base):
        start = number * cap
        local = slot_c - start
        inside = (local >= 0) & (local < cap)
        key = jnp.where(inside, class_c * cap + local, -1)
        right_high, right_low = compact(cycle, key[:, :, None], cap)
        left = sort_rows(doubles, place_r[None, :], n_occ, chunks, n)
        at = lambda x, index: lax.dynamic_index_in_dim(x, index, 0, keepdims=False)
        here = jnp.bitwise_xor(col_pos, row_pos)
        every = [(m, h) for m in range(half) for h in range(chunks)]
        swap = [(d, (d + 1) % n_occ) for d in range(n_occ)]
        spread = exchange(
            lambda t: lax.dynamic_index_in_dim(left, jnp.bitwise_xor(col_pos, t), 2, keepdims=False), "col", n
        )
        spread, right_high, right_low = after(spread, right_high, right_low)

        def to_plane(spread, k):
            m, h = every[k]
            return exchange(lambda t: at(spread[:, m, h], jnp.bitwise_xor(here, t)), "row", n)[None]

        def gather(near):
            bits = 2
            while bits < n:
                near = jnp.concatenate([near, flipped(near, "col", n, bits)])
                bits *= 2
            return near

        def multiply(k, near, far, right, which):
            m, h = every[k]
            scalars = jnp.stack([which, row_pos, col_pos, occ_irrep[which * half + m]]).astype(jnp.int32)
            scalars = jnp.concatenate([scalars, has[h]])
            return product(scalars, row_irrep[:, h], near, far, *right, cap)

        live = {"spread": spread, "right": (right_high, right_low)}
        for step in range(len(every) + 3):
            new = dict(live)
            for stage in range(4):
                k = step - stage
                if not 0 <= k < len(every):
                    continue
                if stage == 0:
                    new["near", k] = to_plane(live["spread"], k)
                elif stage == 1:
                    new["full", k] = gather(live["near", k])
                    del new["near", k]
                elif stage == 2:
                    left_rows = live["full", k], flipped(live["full", k], "col", n, 1)
                    new["got", k] = lax.ppermute(multiply(k, *left_rows, live["right"], 1 - occ_pos), "occ", swap)
                    new["kept", k] = multiply(k, *left_rows, live["right"], occ_pos)
                    del new["full", k]
                else:
                    total = (live["kept", k] + live["got", k]).reshape(n, n * sub, cap)
                    new["part", k] = lax.psum_scatter(total, "row", scatter_dimension=0, tiled=True)[0]
                    del new["kept", k], new["got", k]
            if step == len(every) - 1:
                del new["spread"]
            names = list(new)
            live = dict(zip(names, lax.optimization_barrier(tuple(new[name] for name in names))))
        own = jnp.concatenate([live["part", k] for k in range(len(every))], axis=0).reshape(half, tile_a, cap)
        swapped = lax.ppermute(own, "occ", swap)
        turned = turn(own.reshape(half, n, tile_a // n, cap).transpose(1, 0, 2, 3), n).transpose(1, 0, 2, 3)
        turned = turned.reshape(half, tile_a, cap)
        tables = (occ_pos.reshape(1), own_j(local), (slot_r - start)[:, :, None]) + fixed
        shape = (n_i, tile_a, half, tile_b)
        return finish(tables, own, swapped, turned, base, cap, shape)

    first = one_round(doubles, cycle, jnp.int32(0), None)

    def more(state):
        number, total, doubles, cycle = state
        return number + 1, one_round(doubles, cycle, number, total), doubles, cycle

    state = (jnp.int32(1), first, doubles, cycle)
    return lax.while_loop(lambda state: state[0] < rounds, more, state)[1]


def solution(mesh):
    return jax.shard_map(
        shards,
        mesh=mesh,
        in_specs=(P(None, "row", "occ", "col"), P("occ", "row", None, "col"), P(), P(), P()),
        out_specs=P(None, "row", "occ", "col"),
        check_vma=False,
    )
```

time: 2050 us -> 887 us (0.43)
  waiting for transfers between devices: 1270 us -> 415 us
  blocking collectives: 379 us -> 34.6 us
  matrix products: 222 us -> 0 us
  Pallas kernels: 0 us -> 208 us
  local copies, waits for them, and re-layouts: 149 us -> 69.9 us
  starting transfers between devices: 5.85 us -> 65.1 us
  other arithmetic: 11.1 us -> 60.6 us
    all_gather x2 -> x0, waiting for transfers between devices: 708 us -> none  [the longest x1 565 us: shards(): lax.all_gather(cycle, 'row', axis=1, tiled=True)]
    unnamed x4, waiting for transfers between devices: 378 us -> 0.07 us
    all_to_all x3 -> x1, blocking collectives: 379 us -> 34.6 us  [turn(): x = lax.all_to_all(x, axis, split_axis=0, concat_axis=0, tiled=True)]
    ppermute x0 -> x28, waiting for transfers between devices: none -> 259 us  [the longest x23 232 us: flipped(): return lax.ppermute(x, axis, [(d, d ^ bits) for d in range(n)])]
    dot_general x1 -> x0, matrix products: 222 us -> none  [contract(): jnp.dot(left_part.reshape(n_i * tile_a, k_part * c_part), right_part.resh...]
    pallas_call x0 -> x11, Pallas kernels: none -> 208 us  [the longest x8 135 us: product(): pl.pallas_call(functools.partial(product_body, cap), out_shape=jax.ShapeD...]
    all_to_all x1 -> x2, waiting for transfers between devices: 180 us -> 74.2 us  [turn(): x = lax.all_to_all(x, axis, split_axis=0, concat_axis=0, tiled=True)]
    reduce_scatter x0 -> x4, waiting for transfers between devices: none -> 82 us  [one_round(): lax.psum_scatter(total, 'row', scatter_dimension=0, tiled=True)[0]]
  transfers between devices with their start and end apart: 4 -> 34, of which waited for: 4 -> 20; matrix products, arithmetic and copies ran while one was open for 3% -> 9% of each run, Pallas kernels for 0% -> 20%
where the time goes in v1:
time: 887 us; the launch traced here: 877 us
  waiting for transfers between devices  415 us (47%)
  Pallas kernels  208 us (23%)
  local copies, waits for them, and re-layouts  69.9 us (8%)
  starting transfers between devices  65.1 us (7%)
  other arithmetic  60.6 us (7%)
  blocking collectives  34.6 us (4%)
  between operations  22.2 us (3%)
    ppermute x23, waiting for transfers between devices, flipped(): return lax.ppermute(x, axis, [(d, d ^ bits) for d in range(n)])  232 us
    pallas_call x8, Pallas kernels, product(): pl.pallas_call(functools.partial(product_body, cap), out_shape=jax.ShapeD...  135 us
    reduce_scatter x4, waiting for transfers between devices, one_round(): lax.psum_scatter(total, 'row', scatter_dimension=0, tiled=True)[0]  82 us
    all_to_all x2, waiting for transfers between devices, turn(): x = lax.all_to_all(x, axis, split_axis=0, concat_axis=0, tiled=True)  74.2 us
    ppermute x23, starting transfers between devices, flipped(): return lax.ppermute(x, axis, [(d, d ^ bits) for d in range(n)])  50.3 us
    pallas_call x1, Pallas kernels, compact(): pl.pallas_call(functools.partial(compact_body, cap), out_shape=(out, out)...  36.4 us
    all_to_all x1, blocking collectives, turn(): x = lax.all_to_all(x, axis, split_axis=0, concat_axis=0, tiled=True)  34.6 us
    ppermute x4, waiting for transfers between devices, one_round(): lax.ppermute(multiply(k, *left_rows, live['right'], 1 - occ_pos), 'occ',...  27.6 us
  transfers between devices with their start and end apart: 34, of which 20 were waited for; matrix products, arithmetic and copies ran while one was open for 9% of the time, Pallas kernels for 20%

profile of v1, /device:TPU:0, one launch (start us, length us, event | category | flops | bytes accessed | tf_op | source)
XLA Modules:
  0.0 876.6 jit_solution(16259113271335694365)
XLA Ops:
  17.4 3.2 fusion.59
  22.0 11.8 %reshape.780.rows_ref = f32[4,512,1024]{2,1,0:T(8,128)} reshape(f32[4,512,2,512]{3,2,1,0:T(2,128)} %param.7) | data formatting | bytes 16777216 | tf_op jit(solution)/shard_map/reshape | solution.py:51
  33.8 5.6 fusion.68
  39.4 9.4 %shard_map.55 = f32[2,2,4,2,64,1024]{5,4,3,2,1,0:T(8,128)} custom-call(s32[1,512]{1,0:T(1,128)} %get-tuple-element.1187.place_ref, f32[4,512,1024]{2,1,0:T(8,128)} %reshape.780.rows_ref), custom_call_target="tpu_custom_call" | custom-call | flops 4294967296 | bytes 16777216 | tf_op jit(solution)/shard_map/pallas_call | solution.py:38
  48.8 6.8 dynamic-slice_bitcast_fusion.19
  67.1 10.9 %copy.287 = f32[128,8,4,512]{3,1,2,0:T(8,128)} copy(f32[128,8,4,512]{3,2,1,0:T(4,128)} %bitcast.296) | data formatting | bytes 16777216
  78.0 36.4 %shard_map.56 = (bf16[1024,2560]{1,0:T(8,128)(2,1)}, bf16[1024,2560]{1,0:T(8,128)(2,1)}) custom-call(s32[4,512,1]{2,1,0:T(8,128)} %and_select_fusion.key_ref, f32[1024,2048]{1,0:T(8,128)} %bitcast.326), custom_call_target="tpu_custom_call" | custom-call | flops 21474836480 | bytes 8388608 | tf_op jit(solution)/shard_map/pallas_call | solution.py:85
  114.5 35.4 %collective-permute-done.27 = f32[2,2,2,64,1024]{4,3,2,1,0:T(8,128)} collective-permute-done((f32[2,2,2,64,1024]{4,3,2,1,0:T(8,128)}, f32[2,2,2,64,1024]{4,3,2,1,0:T(8,128)}, u32[]{:S(2)}, u32[]{:S(2)}) %collective-permute-start.27) | collective-permute-done | bytes 2097184 | tf_op jit(solution)/shard_map/ppermute | solution.py:247
  149.9 3.2 pad_maximum_fusion.4
  158.1 20.2 %collective-permute-done.28 = f32[2,64,1024]{2,1,0:T(8,128)S(1)} collective-permute-done((f32[2,64,1024]{2,1,0:T(8,128)S(1)}, f32[2,64,1024]{2,1,0:T(8,128)S(1)}, u32[]{:S(2)}, u32[]{:S(2)}) %collective-permute-start.28) | collective-permute-done | bytes 524320 | tf_op jit(solution)/shard_map/ppermute | solution.py:247
  178.3 15.1 %collective-permute-done.29 = f32[2,64,1024]{2,1,0:T(8,128)S(1)} collective-permute-done((f32[2,64,1024]{2,1,0:T(8,128)S(1)}, f32[2,64,1024]{2,1,0:T(8,128)S(1)}, u32[]{:S(2)}, u32[]{:S(2)}) %collective-permute-start.29) | collective-permute-done | bytes 524320 | tf_op jit(solution)/shard_map/ppermute | solution.py:247
  195.8 10.9 %collective-permute-start.31 = (f32[2,64,1024]{2,1,0:T(8,128)S(1)}, f32[2,64,1024]{2,1,0:T(8,128)S(1)}, u32[]{:S(2)}, u32[]{:S(2)}) collective-permute-start(f32[2,64,1024]{2,1,0:T(8,128)S(1)} %get-tuple-element.1224), channel_id=1, source_target_pairs={{0,8},{8,0},{16,24},{24,16},{1,9},{9,1},{17,25},{25,17},{2,10},{10... | collective-permute-start | bytes 1572872 | tf_op jit(solution)/shard_map/ppermute | solution.py:247
  209.1 18.4 %collective-permute-done.31 = f32[2,64,1024]{2,1,0:T(8,128)S(1)} collective-permute-done((f32[2,64,1024]{2,1,0:T(8,128)S(1)}, f32[2,64,1024]{2,1,0:T(8,128)S(1)}, u32[]{:S(2)}, u32[]{:S(2)}) %collective-permute-start.31) | collective-permute-done | bytes 524320 | tf_op jit(solution)/shard_map/ppermute | solution.py:247
  227.5 17.4 %collective-permute-done.32 = f32[2,64,1024]{2,1,0:T(8,128)S(1)} collective-permute-done((f32[2,64,1024]{2,1,0:T(8,128)S(1)}, f32[2,64,1024]{2,1,0:T(8,128)S(1)}, u32[]{:S(2)}, u32[]{:S(2)}) %collective-permute-start.32) | collective-permute-done | bytes 524320 | tf_op jit(solution)/shard_map/ppermute | solution.py:247
  251.7 3.3 collective-permute-done.39.far_ref
  255.0 16.1 %shard_map.57 = f32[4,4,64,640]{3,2,1,0:T(8,128)} custom-call(s32[20]{0:T(128)S(1)} %concatenate.102.scalar_ref, s32[4,4,64,1]{3,2,1,0:T(8,128)} %copy.265.irrep_ref, f32[2,4,2,64,1024]{4,3,2,1,0:T(8,128)} %pad_maximum_fusion.5.near_ref, f32[2,4,2,64,1024]{4,3,2,1,0:T(8,128)} %collective-permute-done.39.far_ref, ...), custom_call_target="tpu_custom_call" | custom-call | flops 8053063680 | bytes 14680064 | tf_op jit(solution)/shard_map/pallas_call | solution.py:146
  275.6 9.4 %collective-permute-start.35 = (f32[2,64,1024]{2,1,0:T(8,128)}, f32[2,64,1024]{2,1,0:T(8,128)}, u32[]{:S(2)}, u32[]{:S(2)}) collective-permute-start(f32[2,64,1024]{2,1,0:T(8,128)} %get-tuple-element.1220), channel_id=1, source_target_pairs={{0,8},{8,0},{16,24},{24,16},{1,9},{9,1},{17,25},{25,17},{2,10},{10... | collective-permute-start | bytes 1572872 | tf_op jit(solution)/shard_map/ppermute | solution.py:247
  288.2 19.5 %collective-permute-done.35 = f32[2,64,1024]{2,1,0:T(8,128)} collective-permute-done((f32[2,64,1024]{2,1,0:T(8,128)}, f32[2,64,1024]{2,1,0:T(8,128)}, u32[]{:S(2)}, u32[]{:S(2)}) %collective-permute-start.35) | collective-permute-done | bytes 524320 | tf_op jit(solution)/shard_map/ppermute | solution.py:247
  307.7 15.8 %collective-permute-done.36 = f32[2,64,1024]{2,1,0:T(8,128)} collective-permute-done((f32[2,64,1024]{2,1,0:T(8,128)}, f32[2,64,1024]{2,1,0:T(8,128)}, u32[]{:S(2)}, u32[]{:S(2)}) %collective-permute-start.36) | collective-permute-done | bytes 524320 | tf_op jit(solution)/shard_map/ppermute | solution.py:247
  323.5 2.9 maximum_bitcast_fusion.6
  326.4 4.0 pad_maximum_fusion.6.near_ref
  330.3 16.2 %shard_map.58 = f32[4,4,64,640]{3,2,1,0:T(8,128)} custom-call(s32[20]{0:T(128)S(1)} %concatenate.103.scalar_ref, s32[4,4,64,1]{3,2,1,0:T(8,128)} %copy.265.irrep_ref, f32[2,4,2,64,1024]{4,3,2,1,0:T(8,128)} %pad_maximum_fusion.5.near_ref, f32[2,4,2,64,1024]{4,3,2,1,0:T(8,128)} %collective-permute-done.39.far_ref, ...), custom_call_target="tpu_custom_call" | custom-call | flops 8053063680 | bytes 14680064 | tf_op jit(solution)/shard_map/pallas_call | solution.py:146
  346.6 4.4 add.701
  354.1 17.9 %shard_map.59 = f32[4,4,64,640]{3,2,1,0:T(8,128)} custom-call(s32[20]{0:T(128)S(1)} %concatenate.105.scalar_ref, s32[4,4,64,1]{3,2,1,0:T(8,128)} %copy.267.irrep_ref, f32[2,4,2,64,1024]{4,3,2,1,0:T(8,128)} %pad_maximum_fusion.6.near_ref, f32[2,4,2,64,1024]{4,3,2,1,0:T(8,128)} %collective-permute-done.45.far_ref, ...), custom_call_target="tpu_custom_call" | custom-call | flops 8053063680 | bytes 14680064 | tf_op jit(solution)/shard_map/pallas_call | solution.py:146
  375.5 10.9 %collective-permute-start.41 = (f32[2,64,1024]{2,1,0:T(8,128)}, f32[2,64,1024]{2,1,0:T(8,128)}, u32[]{:S(2)}, u32[]{:S(2)}) collective-permute-start(f32[2,64,1024]{2,1,0:T(8,128)} %get-tuple-element.1216), channel_id=1, source_target_pairs={{0,8},{8,0},{16,24},{24,16},{1,9},{9,1},{17,25},{25,17},{2,10},{10... | collective-permute-start | bytes 1572872 | tf_op jit(solution)/shard_map/ppermute | solution.py:247
  389.6 41.5 %collective-permute-done.41 = f32[2,64,1024]{2,1,0:T(8,128)} collective-permute-done((f32[2,64,1024]{2,1,0:T(8,128)}, f32[2,64,1024]{2,1,0:T(8,128)}, u32[]{:S(2)}, u32[]{:S(2)}) %collective-permute-start.41) | collective-permute-done | bytes 524320 | tf_op jit(solution)/shard_map/ppermute | solution.py:247
  431.1 13.4 %collective-permute-done.43 = f32[2,64,1024]{2,1,0:T(8,128)} collective-permute-done((f32[2,64,1024]{2,1,0:T(8,128)S(1)}, f32[2,64,1024]{2,1,0:T(8,128)}, u32[]{:S(2)}, u32[]{:S(2)}) %collective-permute-start.43) | collective-permute-done | bytes 524320 | tf_op jit(solution)/shard_map/ppermute | solution.py:247
  447.4 4.0 pad_maximum_fusion.7.near_ref
  451.4 17.4 %shard_map.60 = f32[4,4,64,640]{3,2,1,0:T(8,128)} custom-call(s32[20]{0:T(128)S(1)} %concatenate.106.scalar_ref, s32[4,4,64,1]{3,2,1,0:T(8,128)} %copy.267.irrep_ref, f32[2,4,2,64,1024]{4,3,2,1,0:T(8,128)} %pad_maximum_fusion.6.near_ref, f32[2,4,2,64,1024]{4,3,2,1,0:T(8,128)} %collective-permute-done.45.far_ref, ...), custom_call_target="tpu_custom_call" | custom-call | flops 8053063680 | bytes 14680064 | tf_op jit(solution)/shard_map/pallas_call | solution.py:146
  468.9 4.3 add.706
  476.4 16.1 %shard_map.61 = f32[4,4,64,640]{3,2,1,0:T(8,128)} custom-call(s32[20]{0:T(128)S(1)} %concatenate.108.scalar_ref, s32[4,4,64,1]{3,2,1,0:T(8,128)} %copy.265.irrep_ref, f32[2,4,2,64,1024]{4,3,2,1,0:T(8,128)} %pad_maximum_fusion.7.near_ref, f32[2,4,2,64,1024]{4,3,2,1,0:T(8,128)} %collective-permute-done.48.far_ref, ...), custom_call_target="tpu_custom_call" | custom-call | flops 8053063680 | bytes 14680064 | tf_op jit(solution)/shard_map/pallas_call | solution.py:146
  494.6 28.4 %collective-permute-done.47 = f32[1,4,2,64,1024]{4,3,2,1,0:T(8,128)} collective-permute-done((f32[1,4,2,64,1024]{4,3,2,1,0:T(8,128)S(1)}, f32[1,4,2,64,1024]{4,3,2,1,0:T(8,128)}, u32[]{:S(2)}, u32[]{:S(2)}) %collective-permute-start.47) | collective-permute-done | bytes 2097184 | tf_op jit(solution)/shard_map/ppermute | solution.py:247
  523.0 4.0 pad_maximum_fusion.8.near_ref
  526.9 16.1 %shard_map.62 = f32[4,4,64,640]{3,2,1,0:T(8,128)} custom-call(s32[20]{0:T(128)S(1)} %concatenate.109.scalar_ref, s32[4,4,64,1]{3,2,1,0:T(8,128)} %copy.265.irrep_ref, f32[2,4,2,64,1024]{4,3,2,1,0:T(8,128)} %pad_maximum_fusion.7.near_ref, f32[2,4,2,64,1024]{4,3,2,1,0:T(8,128)} %collective-permute-done.48.far_ref, ...), custom_call_target="tpu_custom_call" | custom-call | flops 8053063680 | bytes 14680064 | tf_op jit(solution)/shard_map/pallas_call | solution.py:146
  543.1 8.7 collective-permute-done.49
  551.8 4.4 add.707
  559.3 17.7 %shard_map.63 = f32[4,4,64,640]{3,2,1,0:T(8,128)} custom-call(s32[20]{0:T(128)S(1)} %concatenate.110.scalar_ref, s32[4,4,64,1]{3,2,1,0:T(8,128)} %copy.267.irrep_ref, f32[2,4,2,64,1024]{4,3,2,1,0:T(8,128)} %pad_maximum_fusion.8.near_ref, f32[2,4,2,64,1024]{4,3,2,1,0:T(8,128)} %collective-permute-done.50.far_ref, ...), custom_call_target="tpu_custom_call" | custom-call | flops 8053063680 | bytes 14680064 | tf_op jit(solution)/shard_map/pallas_call | solution.py:146
  579.1 17.6 %shard_map.64 = f32[4,4,64,640]{3,2,1,0:T(8,128)} custom-call(s32[20]{0:T(128)S(1)} %concatenate.111.scalar_ref, s32[4,4,64,1]{3,2,1,0:T(8,128)} %copy.267.irrep_ref, f32[2,4,2,64,1024]{4,3,2,1,0:T(8,128)} %pad_maximum_fusion.8.near_ref, f32[2,4,2,64,1024]{4,3,2,1,0:T(8,128)} %collective-permute-done.50.far_ref, ...), custom_call_target="tpu_custom_call" | custom-call | flops 8053063680 | bytes 14680064 | tf_op jit(solution)/shard_map/pallas_call | solution.py:146
  596.7 20.5 %reduce-scatter.13.cloned.1.call-done = f32[1,256,640]{2,1,0:T(8,128)} async-done(((f32[4,256,640]{2,1,0:T(8,128)}), f32[1,256,640]{2,1,0:T(8,128)}) %reduce-scatter.13.cloned.1.call-update) | async-done | bytes 655376 | tf_op jit(solution)/shard_map/reduce_scatter | solution.py:364
  617.2 18.9 %collective-permute-done.51 = f32[4,4,64,640]{3,2,1,0:T(8,128)S(1)} collective-permute-done((f32[4,4,64,640]{3,2,1,0:T(8,128)}, f32[4,4,64,640]{3,2,1,0:T(8,128)S(1)}, u32[]{:S(2)}, u32[]{:S(2)}) %collective-permute-start.51) | collective-permute-done | bytes 2621472 | tf_op jit(solution)/shard_map/ppermute | solution.py:359
  636.0 3.5 add.708
  639.6 61.5 %reduce-scatter.15.cloned.1.call-done = f32[1,256,640]{2,1,0:T(8,128)} async-done(((f32[4,256,640]{2,1,0:T(8,128)}), f32[1,256,640]{2,1,0:T(8,128)}) %reduce-scatter.15.cloned.1.call-update) | async-done | bytes 655376 | tf_op jit(solution)/shard_map/reduce_scatter | solution.py:364
  706.6 34.6 %all_to_all.48 = f32[4,2,128,640]{3,2,1,0:T(8,128)} all-to-all(f32[4,2,128,640]{3,2,1,0:T(8,128)S(1)} %copy.273), channel_id=1, replica_groups=mesh['row'=4,'col'=4,'occ'=2] {'col'}, dimensions={0} | all-to-all | bytes 5242880 | tf_op jit(solution)/shard_map/all_to_all | solution.py:256
  741.2 4.6 all-to-all-start.4
  747.4 57.8 %all-to-all-done.4 = f32[4,2,128,640]{3,2,1,0:T(8,128)} async-done(((f32[4,2,128,640]{3,2,1,0:T(8,128)}), f32[4,2,128,640]{3,2,1,0:T(8,128)}, u32[]{:S(2)}, u32[]{:S(2)}) %all-to-all-start.4) | async-done | bytes 2621472 | tf_op jit(solution)/shard_map/all_to_all | solution.py:256
  805.2 3.7 all-to-all-start.5
  823.7 16.4 %all-to-all-done.5 = f32[4,2,128,640]{3,2,1,0:T(8,128)S(1)} async-done(((f32[4,2,128,640]{3,2,1,0:T(8,128)}), f32[4,2,128,640]{3,2,1,0:T(8,128)S(1)}, u32[]{:S(2)}, u32[]{:S(2)}) %all-to-all-start.5) | async-done | bytes 2621472 | tf_op jit(solution)/shard_map/all_to_all | solution.py:256
  842.0 26.8 %shard_map.65 = f32[4,512,2,512]{3,2,1,0:T(2,128)} custom-call(s32[1]{0:T(128)} %bitcast.occ_pos_ref, s32[2,512]{1,0:T(2,128)} %constant_dynamic-slice_fusion.5.key_c_ref, s32[4,512,1]{2,1,0:T(8,128)} %copy.275.slot_r_ref, s32[4]{0:T(128)S(1)} %slice.137.irrep_i_ref, s32[512,1]{1,0:T(8,128)S(1)} %copy-done.18, s32[512,1]{1,0:T(8,128)S(1)} %copy-done.14, ...), custom_call_target="tpu_custom_call" | custom-call | flops 10737418240 | bytes 13631488 | tf_op jit(solution)/shard_map/pallas_call | solution.py:222
  (224 shorter events, 87.6 us)
Async XLA Ops:
  6.5 462.3 %reduce-scatter.9.cloned.1.call-start = ((), (), s32[]{:S(2)}) async-start(), calls=%async_computation.14 | async-start | bytes 3276800 | tf_op jit(solution)/shard_map/reduce_scatter | solution.py:364
  55.6 58.9 %collective-permute-start.25 = (f32[2,2,2,64,1024]{4,3,2,1,0:T(8,128)}, f32[2,2,2,64,1024]{4,3,2,1,0:T(8,128)}, u32[]{:S(2)}, u32[]{:S(2)}) collective-permute-start(f32[2,2,2,64,1024]{4,3,2,1,0:T(8,128)} %get-tuple-element.1212), channel_id=1, source_target_pairs={{0,2},{2,0},{4,6},{6,4},{1,3},{3,1},{5,7},{7,5},{8,10},{10,8},{12,... | collective-permute-start | bytes 6291464 | tf_op jit(solution)/shard_map/ppermute | solution.py:247
  56.0 58.4 %collective-permute-start.26 = (f32[2,2,2,64,1024]{4,3,2,1,0:T(8,128)}, f32[2,2,2,64,1024]{4,3,2,1,0:T(8,128)}, u32[]{:S(2)}, u32[]{:S(2)}) collective-permute-start(f32[2,2,2,64,1024]{4,3,2,1,0:T(8,128)} %get-tuple-element.1211), channel_id=1, source_target_pairs={{0,4},{2,6},{4,0},{6,2},{1,5},{3,7},{5,1},{7,3},{8,12},{10,14},{12... | collective-permute-start | bytes 6291464 | tf_op jit(solution)/shard_map/ppermute | solution.py:247
  58.5 91.4 %collective-permute-start.27 = (f32[2,2,2,64,1024]{4,3,2,1,0:T(8,128)}, f32[2,2,2,64,1024]{4,3,2,1,0:T(8,128)}, u32[]{:S(2)}, u32[]{:S(2)}) collective-permute-start(f32[2,2,2,64,1024]{4,3,2,1,0:T(8,128)} %get-tuple-element.1210), channel_id=1, source_target_pairs={{0,6},{2,4},{4,2},{6,0},{1,7},{3,5},{5,3},{7,1},{8,14},{10,12},{12... | collective-permute-start | bytes 6291464 | tf_op jit(solution)/shard_map/ppermute | solution.py:247
  153.1 42.2 %copy-start = (f32[4,2,2,2,64,1024]{5,4,3,2,1,0:T(8,128)}, f32[4,2,2,2,64,1024]{5,4,3,2,1,0:T(8,128)S(1)}, u32[]{:S(2)}) copy-start(f32[4,2,2,2,64,1024]{5,4,3,2,1,0:T(8,128)S(1)} %pad_maximum_fusion.4) | copy-start | bytes 25165828
  153.6 24.7 %collective-permute-start.28 = (f32[2,64,1024]{2,1,0:T(8,128)S(1)}, f32[2,64,1024]{2,1,0:T(8,128)S(1)}, u32[]{:S(2)}, u32[]{:S(2)}) collective-permute-start(f32[2,64,1024]{2,1,0:T(8,128)S(1)} %get-tuple-element.1228), channel_id=1, source_target_pairs={{0,8},{8,0},{16,24},{24,16},{1,9},{9,1},{17,25},{25,17},{2,10},{10... | collective-permute-start | bytes 1572872 | tf_op jit(solution)/shard_map/ppermute | solution.py:247
  155.3 38.2 %collective-permute-start.29 = (f32[2,64,1024]{2,1,0:T(8,128)S(1)}, f32[2,64,1024]{2,1,0:T(8,128)S(1)}, u32[]{:S(2)}, u32[]{:S(2)}) collective-permute-start(f32[2,64,1024]{2,1,0:T(8,128)S(1)} %get-tuple-element.1227), channel_id=1, source_target_pairs={{0,16},{8,24},{16,0},{24,8},{1,17},{9,25},{17,1},{25,9},{2,18},{10... | collective-permute-start | bytes 1572872 | tf_op jit(solution)/shard_map/ppermute | solution.py:247
  157.9 35.6 %collective-permute-start.30 = (f32[2,64,1024]{2,1,0:T(8,128)S(1)}, f32[2,64,1024]{2,1,0:T(8,128)S(1)}, u32[]{:S(2)}, u32[]{:S(2)}) collective-permute-start(f32[2,64,1024]{2,1,0:T(8,128)S(1)} %get-tuple-element.1226), channel_id=1, source_target_pairs={{0,24},{8,16},{16,8},{24,0},{1,25},{9,17},{17,9},{25,1},{2,26},{10... | collective-permute-start | bytes 1572872 | tf_op jit(solution)/shard_map/ppermute | solution.py:247
  193.7 51.4 %collective-permute-start.34 = (f32[1,4,2,64,1024]{4,3,2,1,0:T(8,128)S(1)}, f32[1,4,2,64,1024]{4,3,2,1,0:T(8,128)S(1)}, u32[]{:S(2)}, u32[]{:S(2)}) collective-permute-start(f32[1,4,2,64,1024]{4,3,2,1,0:T(8,128)S(1)} %maximum_bitcast_fusion.4), channel_id=1, source_target_pairs={{0,4},{2,6},{4,0},{6,2},{1,5},{3,7},{5,1},{7,3},{8,12},{10,14},{12... | collective-permute-start | bytes 6291464 | tf_op jit(solution)/shard_map/ppermute | solution.py:247
  195.8 31.7 %collective-permute-start.31 = (f32[2,64,1024]{2,1,0:T(8,128)S(1)}, f32[2,64,1024]{2,1,0:T(8,128)S(1)}, u32[]{:S(2)}, u32[]{:S(2)}) collective-permute-start(f32[2,64,1024]{2,1,0:T(8,128)S(1)} %get-tuple-element.1224), channel_id=1, source_target_pairs={{0,8},{8,0},{16,24},{24,16},{1,9},{9,1},{17,25},{25,17},{2,10},{10... | collective-permute-start | bytes 1572872 | tf_op jit(solution)/shard_map/ppermute | solution.py:247
  206.7 38.2 %collective-permute-start.32 = (f32[2,64,1024]{2,1,0:T(8,128)S(1)}, f32[2,64,1024]{2,1,0:T(8,128)S(1)}, u32[]{:S(2)}, u32[]{:S(2)}) collective-permute-start(f32[2,64,1024]{2,1,0:T(8,128)S(1)} %get-tuple-element.1223), channel_id=1, source_target_pairs={{0,16},{8,24},{16,0},{24,8},{1,17},{9,25},{17,1},{25,9},{2,18},{10... | collective-permute-start | bytes 1572872 | tf_op jit(solution)/shard_map/ppermute | solution.py:247
  207.8 37.1 %collective-permute-start.33 = (f32[2,64,1024]{2,1,0:T(8,128)S(1)}, f32[2,64,1024]{2,1,0:T(8,128)S(1)}, u32[]{:S(2)}, u32[]{:S(2)}) collective-permute-start(f32[2,64,1024]{2,1,0:T(8,128)S(1)} %get-tuple-element.1222), channel_id=1, source_target_pairs={{0,24},{8,16},{16,8},{24,0},{1,25},{9,17},{17,9},{25,1},{2,26},{10... | collective-permute-start | bytes 1572872 | tf_op jit(solution)/shard_map/ppermute | solution.py:247
  247.5 7.5 collective-permute-start.39
  251.2 75.2 %collective-permute-start.38 = (f32[1,4,2,64,1024]{4,3,2,1,0:T(8,128)S(1)}, f32[1,4,2,64,1024]{4,3,2,1,0:T(8,128)}, u32[]{:S(2)}, u32[]{:S(2)}) collective-permute-start(f32[1,4,2,64,1024]{4,3,2,1,0:T(8,128)S(1)} %maximum_bitcast_fusion.5), channel_id=1, source_target_pairs={{0,4},{2,6},{4,0},{6,2},{1,5},{3,7},{5,1},{7,3},{8,12},{10,14},{12... | collective-permute-start | bytes 6291464 | tf_op jit(solution)/shard_map/ppermute | solution.py:247
  271.1 75.4 %collective-permute-start.40 = (f32[4,4,64,640]{3,2,1,0:T(8,128)}, f32[4,4,64,640]{3,2,1,0:T(8,128)}, u32[]{:S(2)}, u32[]{:S(2)}) collective-permute-start(f32[4,4,64,640]{3,2,1,0:T(8,128)} %shard_map.57), channel_id=1, source_target_pairs={{0,1},{1,0},{2,3},{3,2},{4,5},{5,4},{6,7},{7,6},{8,9},{9,8},{10,11... | collective-permute-start | bytes 7864328 | tf_op jit(solution)/shard_map/ppermute | solution.py:359
  275.6 32.1 %collective-permute-start.35 = (f32[2,64,1024]{2,1,0:T(8,128)}, f32[2,64,1024]{2,1,0:T(8,128)}, u32[]{:S(2)}, u32[]{:S(2)}) collective-permute-start(f32[2,64,1024]{2,1,0:T(8,128)} %get-tuple-element.1220), channel_id=1, source_target_pairs={{0,8},{8,0},{16,24},{24,16},{1,9},{9,1},{17,25},{25,17},{2,10},{10... | collective-permute-start | bytes 1572872 | tf_op jit(solution)/shard_map/ppermute | solution.py:247
  284.9 38.5 %collective-permute-start.36 = (f32[2,64,1024]{2,1,0:T(8,128)}, f32[2,64,1024]{2,1,0:T(8,128)}, u32[]{:S(2)}, u32[]{:S(2)}) collective-permute-start(f32[2,64,1024]{2,1,0:T(8,128)} %get-tuple-element.1219), channel_id=1, source_target_pairs={{0,16},{8,24},{16,0},{24,8},{1,17},{9,25},{17,1},{25,9},{2,18},{10... | collective-permute-start | bytes 1572872 | tf_op jit(solution)/shard_map/ppermute | solution.py:247
  285.9 37.5 %collective-permute-start.37 = (f32[2,64,1024]{2,1,0:T(8,128)S(1)}, f32[2,64,1024]{2,1,0:T(8,128)}, u32[]{:S(2)}, u32[]{:S(2)}) collective-permute-start(f32[2,64,1024]{2,1,0:T(8,128)S(1)} %get-tuple-element.1218), channel_id=1, source_target_pairs={{0,24},{8,16},{16,8},{24,0},{1,25},{9,17},{17,9},{25,1},{2,26},{10... | collective-permute-start | bytes 1572872 | tf_op jit(solution)/shard_map/ppermute | solution.py:247
  346.6 7.5 collective-permute-start.45
  351.0 192.1 %reduce-scatter.11.cloned.1.call-start = ((), (), s32[]{:S(2)}) async-start(), calls=%async_computation.15 | async-start | bytes 3276800 | tf_op jit(solution)/shard_map/reduce_scatter | solution.py:364
  352.8 94.6 %collective-permute-start.44 = (f32[1,4,2,64,1024]{4,3,2,1,0:T(8,128)S(1)}, f32[1,4,2,64,1024]{4,3,2,1,0:T(8,128)}, u32[]{:S(2)}, u32[]{:S(2)}) collective-permute-start(f32[1,4,2,64,1024]{4,3,2,1,0:T(8,128)S(1)} %copy-done.6), channel_id=1, source_target_pairs={{0,4},{2,6},{4,0},{6,2},{1,5},{3,7},{5,1},{7,3},{8,12},{10,14},{12... | collective-permute-start | bytes 6291464 | tf_op jit(solution)/shard_map/ppermute | solution.py:247
  372.0 96.8 %collective-permute-start.46 = (f32[4,4,64,640]{3,2,1,0:T(8,128)}, f32[4,4,64,640]{3,2,1,0:T(8,128)}, u32[]{:S(2)}, u32[]{:S(2)}) collective-permute-start(f32[4,4,64,640]{3,2,1,0:T(8,128)} %shard_map.59), channel_id=1, source_target_pairs={{0,1},{1,0},{2,3},{3,2},{4,5},{5,4},{6,7},{7,6},{8,9},{9,8},{10,11... | collective-permute-start | bytes 7864328 | tf_op jit(solution)/shard_map/ppermute | solution.py:359
  375.5 55.6 %collective-permute-start.41 = (f32[2,64,1024]{2,1,0:T(8,128)}, f32[2,64,1024]{2,1,0:T(8,128)}, u32[]{:S(2)}, u32[]{:S(2)}) collective-permute-start(f32[2,64,1024]{2,1,0:T(8,128)} %get-tuple-element.1216), channel_id=1, source_target_pairs={{0,8},{8,0},{16,24},{24,16},{1,9},{9,1},{17,25},{25,17},{2,10},{10... | collective-permute-start | bytes 1572872 | tf_op jit(solution)/shard_map/ppermute | solution.py:247
  386.4 44.7 %collective-permute-start.42 = (f32[2,64,1024]{2,1,0:T(8,128)}, f32[2,64,1024]{2,1,0:T(8,128)}, u32[]{:S(2)}, u32[]{:S(2)}) collective-permute-start(f32[2,64,1024]{2,1,0:T(8,128)} %get-tuple-element.1215), channel_id=1, source_target_pairs={{0,16},{8,24},{16,0},{24,8},{1,17},{9,25},{17,1},{25,9},{2,18},{10... | collective-permute-start | bytes 1572872 | tf_op jit(solution)/shard_map/ppermute | solution.py:247
  387.4 57.1 %collective-permute-start.43 = (f32[2,64,1024]{2,1,0:T(8,128)S(1)}, f32[2,64,1024]{2,1,0:T(8,128)}, u32[]{:S(2)}, u32[]{:S(2)}) collective-permute-start(f32[2,64,1024]{2,1,0:T(8,128)S(1)} %get-tuple-element.1214), channel_id=1, source_target_pairs={{0,24},{8,16},{16,8},{24,0},{1,25},{9,17},{17,9},{25,1},{2,26},{10... | collective-permute-start | bytes 1572872 | tf_op jit(solution)/shard_map/ppermute | solution.py:247
  389.6 61.8 %copy-start.37 = (s32[20]{0:T(128)}, s32[20]{0:T(128)S(1)}, u32[]{:S(2)}) copy-start(s32[20]{0:T(128)S(1)} %concatenate.106.scalar_ref) | copy-start | bytes 244
  468.8 7.6 collective-permute-start.48
  473.3 143.9 %reduce-scatter.13.cloned.1.call-start = ((), (), s32[]{:S(2)}) async-start(), calls=%async_computation.16 | async-start | bytes 3276800 | tf_op jit(solution)/shard_map/reduce_scatter | solution.py:364
  474.8 48.1 %collective-permute-start.47 = (f32[1,4,2,64,1024]{4,3,2,1,0:T(8,128)S(1)}, f32[1,4,2,64,1024]{4,3,2,1,0:T(8,128)}, u32[]{:S(2)}, u32[]{:S(2)}) collective-permute-start(f32[1,4,2,64,1024]{4,3,2,1,0:T(8,128)S(1)} %copy-done.7), channel_id=1, source_target_pairs={{0,4},{2,6},{4,0},{6,2},{1,5},{3,7},{5,1},{7,3},{8,12},{10,14},{12... | collective-permute-start | bytes 6291464 | tf_op jit(solution)/shard_map/ppermute | solution.py:247
  492.5 59.2 %collective-permute-start.49 = (f32[4,4,64,640]{3,2,1,0:T(8,128)}, f32[4,4,64,640]{3,2,1,0:T(8,128)}, u32[]{:S(2)}, u32[]{:S(2)}) collective-permute-start(f32[4,4,64,640]{3,2,1,0:T(8,128)} %shard_map.61), channel_id=1, source_target_pairs={{0,1},{1,0},{2,3},{3,2},{4,5},{5,4},{6,7},{7,6},{8,9},{9,8},{10,11... | collective-permute-start | bytes 7864328 | tf_op jit(solution)/shard_map/ppermute | solution.py:359
  551.8 7.5 collective-permute-start.50
  556.2 144.9 %reduce-scatter.15.cloned.1.call-start = ((), (), s32[]{:S(2)}) async-start(), calls=%async_computation.17 | async-start | bytes 3276800 | tf_op jit(solution)/shard_map/reduce_scatter | solution.py:364
  576.9 59.1 %collective-permute-start.51 = (f32[4,4,64,640]{3,2,1,0:T(8,128)}, f32[4,4,64,640]{3,2,1,0:T(8,128)S(1)}, u32[]{:S(2)}, u32[]{:S(2)}) collective-permute-start(f32[4,4,64,640]{3,2,1,0:T(8,128)} %shard_map.63), channel_id=1, source_target_pairs={{0,1},{1,0},{2,3},{3,2},{4,5},{5,4},{6,7},{7,6},{8,9},{9,8},{10,11... | collective-permute-start | bytes 7864328 | tf_op jit(solution)/shard_map/ppermute | solution.py:359
  639.5 61.5 %copy-start.10 = (f32[1,256,640]{2,1,0:T(8,128)S(1)}, f32[1,256,640]{2,1,0:T(8,128)}, u32[]{:S(2)}) copy-start(f32[1,256,640]{2,1,0:T(8,128)} %reduce-scatter.9.cloned.1.call-done) | copy-start | bytes 1966084
  639.5 62.4 %copy-start.11 = (f32[1,256,640]{2,1,0:T(8,128)S(1)}, f32[1,256,640]{2,1,0:T(8,128)}, u32[]{:S(2)}) copy-start(f32[1,256,640]{2,1,0:T(8,128)} %reduce-scatter.11.cloned.1.call-done) | copy-start | bytes 1966084
  639.6 63.3 %copy-start.12 = (f32[1,256,640]{2,1,0:T(8,128)S(1)}, f32[1,256,640]{2,1,0:T(8,128)}, u32[]{:S(2)}) copy-start(f32[1,256,640]{2,1,0:T(8,128)} %reduce-scatter.13.cloned.1.call-done) | copy-start | bytes 1966084
  741.2 64.0 %all-to-all-start.4 = ((f32[4,2,128,640]{3,2,1,0:T(8,128)}), f32[4,2,128,640]{3,2,1,0:T(8,128)}, u32[]{:S(2)}, u32[]{:S(2)}) async-start(f32[4,2,128,640]{3,2,1,0:T(8,128)} %all_to_all.48), calls=%async_computation.12 | async-start | bytes 5242880 | tf_op jit(solution)/shard_map/all_to_all | solution.py:256
  745.8 63.1 %copy-start.21 = (s32[4,4]{1,0:T(4,128)S(1)}, s32[4,4]{1,0:T(4,128)}, u32[]{:S(2)}) copy-start(s32[4,4]{1,0:T(4,128)} %copy-done.20) | copy-start | bytes 196
  745.8 69.3 %copy-start.24 = (s32[512]{0:T(512)S(1)}, s32[512]{0:T(512)}, u32[]{:S(2)}) copy-start(s32[512]{0:T(512)} %copy-done.23) | copy-start | bytes 6148
  745.8 69.3 %copy-start.27 = (s32[1,512]{1,0:T(1,128)S(1)}, s32[1,512]{1,0:T(1,128)}, u32[]{:S(2)}) copy-start(s32[1,512]{1,0:T(1,128)} %get-tuple-element.1244) | copy-start | bytes 6148
  745.8 69.3 %copy-start.28 = (s32[1,512]{1,0:T(1,128)S(1)}, s32[1,512]{1,0:T(1,128)}, u32[]{:S(2)}) copy-start(s32[1,512]{1,0:T(1,128)} %get-tuple-element.1245) | copy-start | bytes 6148
  745.8 69.3 %copy-start.29 = (s32[1,512]{1,0:T(1,128)S(1)}, s32[1,512]{1,0:T(1,128)}, u32[]{:S(2)}) copy-start(s32[1,512]{1,0:T(1,128)} %get-tuple-element.1246) | copy-start | bytes 6148
  745.8 70.7 %copy-start.26 = (s32[1,512]{1,0:T(1,128)S(1)}, s32[1,512]{1,0:T(1,128)}, u32[]{:S(2)}) copy-start(s32[1,512]{1,0:T(1,128)} %get-tuple-element.1188) | copy-start | bytes 6148
  745.9 71.2 %copy-start.25 = (s32[512,1]{0,1:T(1,128)S(1)}, s32[512,1]{0,1:T(1,128)}, u32[]{:S(2)}) copy-start(s32[512,1]{0,1:T(1,128)} %get-tuple-element.1189) | copy-start | bytes 6148
  745.9 72.8 %copy-start.30 = (f32[2048]{0:T(1024)S(1)}, f32[2048]{0:T(1024)}, u32[]{:S(2)}) copy-start(f32[2048]{0:T(1024)} %param.10) | copy-start | bytes 24580
  745.9 73.7 %copy-start.47 = (f32[4]{0:T(128)S(1)}, f32[4]{0:T(128)}, u32[]{:S(2)}) copy-start(f32[4]{0:T(128)} %param.9) | copy-start | bytes 52
  745.9 95.9 %collective-permute-start.52 = (f32[2,512,640]{2,1,0:T(8,128)}, f32[2,512,640]{2,1,0:T(8,128)}, u32[]{:S(2)}, u32[]{:S(2)}) collective-permute-start(f32[2,512,640]{2,1,0:T(8,128)} %bitcast.93.own_ref), channel_id=1, source_target_pairs={{0,1},{1,0},{2,3},{3,2},{4,5},{5,4},{6,7},{7,6},{8,9},{9,8},{10,11... | collective-permute-start | bytes 7864328 | tf_op jit(solution)/shard_map/ppermute | solution.py:371
  805.2 34.9 %all-to-all-start.5 = ((f32[4,2,128,640]{3,2,1,0:T(8,128)}), f32[4,2,128,640]{3,2,1,0:T(8,128)S(1)}, u32[]{:S(2)}, u32[]{:S(2)}) async-start(f32[4,2,128,640]{3,2,1,0:T(8,128)} %all-to-all-done.4), calls=%async_computation.13 | async-start | bytes 5242880 | tf_op jit(solution)/shard_map/all_to_all | solution.py:256
  (27 other events, 463.8 us)
Sparse Core Ops, SparseCore 0:
  351.1 79.9 reduce-scatter.8
  473.4 60.4 reduce-scatter.10
  556.3 60.8 reduce-scatter.12
  639.7 61.3 reduce-scatter.14

commit v2 on v1

--- a/solution.py
+++ b/solution.py
@@ -103,11 +103,14 @@
 
 
 def product_body(cap, scalar_ref, irrep_ref, near_ref, far_ref, high_ref, low_ref, out_ref, *scratch):
-    left_high_ref, left_low_ref = scratch
+    (both_ref,) = scratch
     n_row, _, sub, depth = near_ref.shape[1:]
+    rows = n_row * sub
     row_pos, col_pos, row_i = scalar_ref[1], scalar_ref[2], scalar_ref[3]
     for at, ref in enumerate((near_ref, far_ref)):
-        left_high_ref[at], left_low_ref[at] = split(ref[0, :, 0].reshape(n_row * sub, depth))
+        high, low = split(ref[0, :, 0].reshape(rows, depth))
+        both_ref[at, :rows] = high
+        both_ref[at, rows:] = low
     out_ref[...] = jnp.zeros_like(out_ref)
 
     @pl.loop(0, 2 * N_IRREPS)
@@ -119,10 +122,8 @@
         @pl.when(scalar_ref[4 + piece * N_IRREPS + irrep] > 0)
         def _():
             span = pl.ds(pl.multiple_of(jnp.bitwise_xor(irrep, row_i) * cap, 128), cap)
-            right_high = high_ref[:, span]
-            left_high = left_high_ref[at]
-            value = dot(left_low_ref[at], right_high) + dot(left_high, low_ref[:, span])
-            value += dot(left_high, right_high)
+            value = dot(both_ref[at], high_ref[:, span])
+            value = value[rows:] + dot(both_ref[at, :rows], low_ref[:, span]) + value[:rows]
             for t in range(n_row):
                 r = jnp.bitwise_xor(row_pos, t)
                 part = value[t * sub : (t + 1) * sub]
@@ -140,7 +141,7 @@
         grid=(n_pair,),
         in_specs=[pl.BlockSpec((n_row, 2, sub, 1), pair), left, left, right, right],
         out_specs=pl.BlockSpec((n_row, 2, sub, cap), pair),
-        scratch_shapes=[pltpu.VMEM((2, n_row * sub, depth), jnp.bfloat16)] * 2,
+        scratch_shapes=[pltpu.VMEM((2, 2 * n_row * sub, depth), jnp.bfloat16)],
     )
     rows = 2 * n_pair * n_row * sub
     return pl.pallas_call(
@@ -251,10 +252,8 @@
     return jnp.stack([pick(0)] + [flipped(pick(t), axis, n, t) for t in range(1, n)])
 
 
-def turn(x, n):
-    for axis in ("col", "row", "col"):
-        x = lax.all_to_all(x, axis, split_axis=0, concat_axis=0, tiled=True)
-    return x
+def spread_out(x, axis):
+    return lax.all_to_all(x, axis, split_axis=0, concat_axis=0, tiled=True)
 
 
 def shards(doubles, cycle, occ_energy, virt_energy, orbital_irrep):
@@ -365,12 +364,16 @@
                     del new["kept", k], new["got", k]
             if step == len(every) - 1:
                 del new["spread"]
+            if step == len(every) + 2:
+                first = [live["part", k].reshape(n, 1, sub, cap) for k in range(len(every) - 1)]
+                new["turned", 0] = spread_out(jnp.concatenate(first, axis=1), "col")
             names = list(new)
             live = dict(zip(names, lax.optimization_barrier(tuple(new[name] for name in names))))
         own = jnp.concatenate([live["part", k] for k in range(len(every))], axis=0).reshape(half, tile_a, cap)
         swapped = lax.ppermute(own, "occ", swap)
-        turned = turn(own.reshape(half, n, tile_a // n, cap).transpose(1, 0, 2, 3), n).transpose(1, 0, 2, 3)
-        turned = turned.reshape(half, tile_a, cap)
+        last = spread_out(live["part", len(every) - 1].reshape(n, 1, sub, cap), "col")
+        turned = jnp.concatenate([live["turned", 0], last], axis=1)
+        turned = spread_out(spread_out(turned, "row"), "col").transpose(1, 0, 2, 3).reshape(half, tile_a, cap)
         tables = (occ_pos.reshape(1), own_j(local), (slot_r - start)[:, :, None]) + fixed
         shape = (n_i, tile_a, half, tile_b)
         return finish(tables, own, swapped, turned, base, cap, shape)

time: 887 us -> 864 us (0.974)
  waiting for transfers between devices: 415 us -> 384 us
    reduce_scatter x4, waiting for transfers between devices: 82 us -> 53.8 us  [one_round(): lax.psum_scatter(total, 'row', scatter_dimension=0, tiled=True)[0]]
    all_to_all x1 -> x2, blocking collectives: 34.6 us -> 40.5 us  [spread_out(): return lax.all_to_all(x, axis, split_axis=0, concat_axis=0, tiled=True)]
  transfers between devices with their start and end apart: 34 -> 34, of which waited for: 20 -> 20; matrix products, arithmetic and copies ran while one was open for 9% -> 10% of each run, Pallas kernels for 20% -> 21%
where the time goes in v2:
time: 864 us; the launch traced here: 855 us
  waiting for transfers between devices  384 us (44%)
  Pallas kernels  212 us (25%)
  local copies, waits for them, and re-layouts  65.9 us (8%)
  starting transfers between devices  65.3 us (8%)
  other arithmetic  64.1 us (7%)
  blocking collectives  40.5 us (5%)
  between operations  22 us (3%)
    ppermute x23, waiting for transfers between devices, flipped(): return lax.ppermute(x, axis, [(d, d ^ bits) for d in range(n)])  230 us
    pallas_call x8, Pallas kernels, product(): pl.pallas_call(functools.partial(product_body, cap), out_shape=jax.ShapeD...  140 us
    all_to_all x2, waiting for transfers between devices, spread_out(): return lax.all_to_all(x, axis, split_axis=0, concat_axis=0, tiled=True)  72.6 us
    reduce_scatter x4, waiting for transfers between devices, one_round(): lax.psum_scatter(total, 'row', scatter_dimension=0, tiled=True)[0]  53.8 us
    ppermute x23, starting transfers between devices, flipped(): return lax.ppermute(x, axis, [(d, d ^ bits) for d in range(n)])  50.3 us
    all_to_all x2, blocking collectives, spread_out(): return lax.all_to_all(x, axis, split_axis=0, concat_axis=0, tiled=True)  40.5 us
    pallas_call x1, Pallas kernels, compact(): pl.pallas_call(functools.partial(compact_body, cap), out_shape=(out, out)...  36.4 us
    ppermute x4, waiting for transfers between devices, one_round(): lax.ppermute(multiply(k, *left_rows, live['right'], 1 - occ_pos), 'occ',...  27.2 us
  transfers between devices with their start and end apart: 34, of which 20 were waited for; matrix products, arithmetic and copies ran while one was open for 10% of the time, Pallas kernels for 21%

profile of v2, /device:TPU:0, one launch (start us, length us, event | category | flops | bytes accessed | tf_op | source)
XLA Modules:
  0.0 854.9 jit_solution(10390206754280423700)
XLA Ops:
  17.2 3.1 fusion.59
  21.8 11.8 %reshape.810.rows_ref = f32[4,512,1024]{2,1,0:T(8,128)} reshape(f32[4,512,2,512]{3,2,1,0:T(2,128)} %param.7) | data formatting | bytes 16777216 | tf_op jit(solution)/shard_map/reshape | solution.py:51
  33.6 5.4 fusion.68
  39.0 9.4 %shard_map.55 = f32[2,2,4,2,64,1024]{5,4,3,2,1,0:T(8,128)} custom-call(s32[1,512]{1,0:T(1,128)} %get-tuple-element.1161.place_ref, f32[4,512,1024]{2,1,0:T(8,128)} %reshape.810.rows_ref), custom_call_target="tpu_custom_call" | custom-call | flops 4294967296 | bytes 16777216 | tf_op jit(solution)/shard_map/pallas_call | solution.py:38
  48.3 6.8 dynamic-slice_bitcast_fusion.19
  67.1 10.9 %copy.240 = f32[128,8,4,512]{3,1,2,0:T(8,128)} copy(f32[128,8,4,512]{3,2,1,0:T(4,128)} %bitcast.304) | data formatting | bytes 16777216
  77.9 36.4 %shard_map.56 = (bf16[1024,2560]{1,0:T(8,128)(2,1)}, bf16[1024,2560]{1,0:T(8,128)(2,1)}) custom-call(s32[4,512,1]{2,1,0:T(8,128)} %and_select_fusion.key_ref, f32[1024,2048]{1,0:T(8,128)} %bitcast.338), custom_call_target="tpu_custom_call" | custom-call | flops 21474836480 | bytes 8388608 | tf_op jit(solution)/shard_map/pallas_call | solution.py:85
  114.3 35.1 %collective-permute-done.27 = f32[2,2,2,64,1024]{4,3,2,1,0:T(8,128)} collective-permute-done((f32[2,2,2,64,1024]{4,3,2,1,0:T(8,128)}, f32[2,2,2,64,1024]{4,3,2,1,0:T(8,128)}, u32[]{:S(2)}, u32[]{:S(2)}) %collective-permute-start.27) | collective-permute-done | bytes 2097184 | tf_op jit(solution)/shard_map/ppermute | solution.py:248
  149.5 3.2 pad_maximum_fusion.7
  157.6 20.2 %collective-permute-done.28 = f32[2,64,1024]{2,1,0:T(8,128)S(1)} collective-permute-done((f32[2,64,1024]{2,1,0:T(8,128)S(1)}, f32[2,64,1024]{2,1,0:T(8,128)S(1)}, u32[]{:S(2)}, u32[]{:S(2)}) %collective-permute-start.28) | collective-permute-done | bytes 524320 | tf_op jit(solution)/shard_map/ppermute | solution.py:248
  177.9 15.1 %collective-permute-done.29 = f32[2,64,1024]{2,1,0:T(8,128)S(1)} collective-permute-done((f32[2,64,1024]{2,1,0:T(8,128)S(1)}, f32[2,64,1024]{2,1,0:T(8,128)S(1)}, u32[]{:S(2)}, u32[]{:S(2)}) %collective-permute-start.29) | collective-permute-done | bytes 524320 | tf_op jit(solution)/shard_map/ppermute | solution.py:248
  195.4 10.9 %collective-permute-start.31 = (f32[2,64,1024]{2,1,0:T(8,128)S(1)}, f32[2,64,1024]{2,1,0:T(8,128)S(1)}, u32[]{:S(2)}, u32[]{:S(2)}) collective-permute-start(f32[2,64,1024]{2,1,0:T(8,128)S(1)} %get-tuple-element.1198), channel_id=1, source_target_pairs={{0,8},{8,0},{16,24},{24,16},{1,9},{9,1},{17,25},{25,17},{2,10},{10... | collective-permute-start | bytes 1572872 | tf_op jit(solution)/shard_map/ppermute | solution.py:248
  208.7 18.4 %collective-permute-done.31 = f32[2,64,1024]{2,1,0:T(8,128)S(1)} collective-permute-done((f32[2,64,1024]{2,1,0:T(8,128)S(1)}, f32[2,64,1024]{2,1,0:T(8,128)S(1)}, u32[]{:S(2)}, u32[]{:S(2)}) %collective-permute-start.31) | collective-permute-done | bytes 524320 | tf_op jit(solution)/shard_map/ppermute | solution.py:248
  227.1 17.4 %collective-permute-done.32 = f32[2,64,1024]{2,1,0:T(8,128)S(1)} collective-permute-done((f32[2,64,1024]{2,1,0:T(8,128)S(1)}, f32[2,64,1024]{2,1,0:T(8,128)S(1)}, u32[]{:S(2)}, u32[]{:S(2)}) %collective-permute-start.32) | collective-permute-done | bytes 524320 | tf_op jit(solution)/shard_map/ppermute | solution.py:248
  251.3 3.2 collective-permute-done.39.far_ref
  254.5 17.4 %shard_map.57 = f32[4,4,64,640]{3,2,1,0:T(8,128)} custom-call(s32[20]{0:T(128)S(1)} %concatenate.120.scalar_ref, s32[4,4,64,1]{3,2,1,0:T(8,128)} %copy.219.irrep_ref, f32[2,4,2,64,1024]{4,3,2,1,0:T(8,128)} %pad_maximum_fusion.8.near_ref, f32[2,4,2,64,1024]{4,3,2,1,0:T(8,128)} %collective-permute-done.39.far_ref, ...), custom_call_target="tpu_custom_call" | custom-call | flops 8053063680 | bytes 14680064 | tf_op jit(solution)/shard_map/pallas_call | solution.py:147
  276.3 9.4 %collective-permute-start.35 = (f32[2,64,1024]{2,1,0:T(8,128)}, f32[2,64,1024]{2,1,0:T(8,128)}, u32[]{:S(2)}, u32[]{:S(2)}) collective-permute-start(f32[2,64,1024]{2,1,0:T(8,128)} %get-tuple-element.1194), channel_id=1, source_target_pairs={{0,8},{8,0},{16,24},{24,16},{1,9},{9,1},{17,25},{25,17},{2,10},{10... | collective-permute-start | bytes 1572872 | tf_op jit(solution)/shard_map/ppermute | solution.py:248
  288.9 19.5 %collective-permute-done.35 = f32[2,64,1024]{2,1,0:T(8,128)} collective-permute-done((f32[2,64,1024]{2,1,0:T(8,128)}, f32[2,64,1024]{2,1,0:T(8,128)}, u32[]{:S(2)}, u32[]{:S(2)}) %collective-permute-start.35) | collective-permute-done | bytes 524320 | tf_op jit(solution)/shard_map/ppermute | solution.py:248
  308.4 15.8 %collective-permute-done.36 = f32[2,64,1024]{2,1,0:T(8,128)} collective-permute-done((f32[2,64,1024]{2,1,0:T(8,128)}, f32[2,64,1024]{2,1,0:T(8,128)}, u32[]{:S(2)}, u32[]{:S(2)}) %collective-permute-start.36) | collective-permute-done | bytes 524320 | tf_op jit(solution)/shard_map/ppermute | solution.py:248
  327.1 4.0 pad_maximum_fusion.9.near_ref
  331.2 17.4 %shard_map.58 = f32[4,4,64,640]{3,2,1,0:T(8,128)} custom-call(s32[20]{0:T(128)S(1)} %concatenate.121.scalar_ref, s32[4,4,64,1]{3,2,1,0:T(8,128)} %copy.219.irrep_ref, f32[2,4,2,64,1024]{4,3,2,1,0:T(8,128)} %pad_maximum_fusion.8.near_ref, f32[2,4,2,64,1024]{4,3,2,1,0:T(8,128)} %collective-permute-done.39.far_ref, ...), custom_call_target="tpu_custom_call" | custom-call | flops 8053063680 | bytes 14680064 | tf_op jit(solution)/shard_map/pallas_call | solution.py:147
  348.6 4.3 add.701
  356.1 17.8 %shard_map.59 = f32[4,4,64,640]{3,2,1,0:T(8,128)} custom-call(s32[20]{0:T(128)S(1)} %concatenate.123.scalar_ref, s32[4,4,64,1]{3,2,1,0:T(8,128)} %copy.221.irrep_ref, f32[2,4,2,64,1024]{4,3,2,1,0:T(8,128)} %pad_maximum_fusion.9.near_ref, f32[2,4,2,64,1024]{4,3,2,1,0:T(8,128)} %collective-permute-done.45.far_ref, ...), custom_call_target="tpu_custom_call" | custom-call | flops 8053063680 | bytes 14680064 | tf_op jit(solution)/shard_map/pallas_call | solution.py:147
  377.4 10.9 %collective-permute-start.41 = (f32[2,64,1024]{2,1,0:T(8,128)}, f32[2,64,1024]{2,1,0:T(8,128)}, u32[]{:S(2)}, u32[]{:S(2)}) collective-permute-start(f32[2,64,1024]{2,1,0:T(8,128)} %get-tuple-element.1190), channel_id=1, source_target_pairs={{0,8},{8,0},{16,24},{24,16},{1,9},{9,1},{17,25},{25,17},{2,10},{10... | collective-permute-start | bytes 1572872 | tf_op jit(solution)/shard_map/ppermute | solution.py:248
  391.5 41.6 %collective-permute-done.41 = f32[2,64,1024]{2,1,0:T(8,128)} collective-permute-done((f32[2,64,1024]{2,1,0:T(8,128)}, f32[2,64,1024]{2,1,0:T(8,128)}, u32[]{:S(2)}, u32[]{:S(2)}) %collective-permute-start.41) | collective-permute-done | bytes 524320 | tf_op jit(solution)/shard_map/ppermute | solution.py:248
  433.1 13.4 %collective-permute-done.43 = f32[2,64,1024]{2,1,0:T(8,128)} collective-permute-done((f32[2,64,1024]{2,1,0:T(8,128)S(1)}, f32[2,64,1024]{2,1,0:T(8,128)}, u32[]{:S(2)}, u32[]{:S(2)}) %collective-permute-start.43) | collective-permute-done | bytes 524320 | tf_op jit(solution)/shard_map/ppermute | solution.py:248
  449.4 4.0 pad_maximum_fusion.10.near_ref
  453.4 17.3 %shard_map.60 = f32[4,4,64,640]{3,2,1,0:T(8,128)} custom-call(s32[20]{0:T(128)S(1)} %concatenate.124.scalar_ref, s32[4,4,64,1]{3,2,1,0:T(8,128)} %copy.221.irrep_ref, f32[2,4,2,64,1024]{4,3,2,1,0:T(8,128)} %pad_maximum_fusion.9.near_ref, f32[2,4,2,64,1024]{4,3,2,1,0:T(8,128)} %collective-permute-done.45.far_ref, ...), custom_call_target="tpu_custom_call" | custom-call | flops 8053063680 | bytes 14680064 | tf_op jit(solution)/shard_map/pallas_call | solution.py:147
  470.8 4.3 add.706
  478.3 17.3 %shard_map.61 = f32[4,4,64,640]{3,2,1,0:T(8,128)} custom-call(s32[20]{0:T(128)S(1)} %concatenate.126.scalar_ref, s32[4,4,64,1]{3,2,1,0:T(8,128)} %copy.219.irrep_ref, f32[2,4,2,64,1024]{4,3,2,1,0:T(8,128)} %pad_maximum_fusion.10.near_ref, f32[2,4,2,64,1024]{4,3,2,1,0:T(8,128)} %collective-permute-done.48.far_ref, ...), custom_call_target="tpu_custom_call" | custom-call | flops 8053063680 | bytes 14680064 | tf_op jit(solution)/shard_map/pallas_call | solution.py:147
  497.7 27.1 %collective-permute-done.47 = f32[1,4,2,64,1024]{4,3,2,1,0:T(8,128)} collective-permute-done((f32[1,4,2,64,1024]{4,3,2,1,0:T(8,128)S(1)}, f32[1,4,2,64,1024]{4,3,2,1,0:T(8,128)}, u32[]{:S(2)}, u32[]{:S(2)}) %collective-permute-start.47) | collective-permute-done | bytes 2097184 | tf_op jit(solution)/shard_map/ppermute | solution.py:248
  524.8 4.0 pad_maximum_fusion.11.near_ref
  528.9 17.5 %shard_map.62 = f32[4,4,64,640]{3,2,1,0:T(8,128)} custom-call(s32[20]{0:T(128)S(1)} %concatenate.127.scalar_ref, s32[4,4,64,1]{3,2,1,0:T(8,128)} %copy.219.irrep_ref, f32[2,4,2,64,1024]{4,3,2,1,0:T(8,128)} %pad_maximum_fusion.10.near_ref, f32[2,4,2,64,1024]{4,3,2,1,0:T(8,128)} %collective-permute-done.48.far_ref, ...), custom_call_target="tpu_custom_call" | custom-call | flops 8053063680 | bytes 14680064 | tf_op jit(solution)/shard_map/pallas_call | solution.py:147
  546.3 8.5 collective-permute-done.49
  554.8 4.3 add.707
  562.3 17.6 %shard_map.63 = f32[4,4,64,640]{3,2,1,0:T(8,128)} custom-call(s32[20]{0:T(128)S(1)} %concatenate.128.scalar_ref, s32[4,4,64,1]{3,2,1,0:T(8,128)} %copy.221.irrep_ref, f32[2,4,2,64,1024]{4,3,2,1,0:T(8,128)} %pad_maximum_fusion.11.near_ref, f32[2,4,2,64,1024]{4,3,2,1,0:T(8,128)} %collective-permute-done.50.far_ref, ...), custom_call_target="tpu_custom_call" | custom-call | flops 8053063680 | bytes 14680064 | tf_op jit(solution)/shard_map/pallas_call | solution.py:147
  582.0 17.4 %shard_map.64 = f32[4,4,64,640]{3,2,1,0:T(8,128)} custom-call(s32[20]{0:T(128)S(1)} %concatenate.129.scalar_ref, s32[4,4,64,1]{3,2,1,0:T(8,128)} %copy.221.irrep_ref, f32[2,4,2,64,1024]{4,3,2,1,0:T(8,128)} %pad_maximum_fusion.11.near_ref, f32[2,4,2,64,1024]{4,3,2,1,0:T(8,128)} %collective-permute-done.50.far_ref, ...), custom_call_target="tpu_custom_call" | custom-call | flops 8053063680 | bytes 14680064 | tf_op jit(solution)/shard_map/pallas_call | solution.py:147
  599.4 20.9 %reduce-scatter.13.cloned.1.call-done = f32[1,256,640]{2,1,0:T(8,128)} async-done(((f32[4,256,640]{2,1,0:T(8,128)}), f32[1,256,640]{2,1,0:T(8,128)}) %reduce-scatter.13.cloned.1.call-update) | async-done | bytes 655376 | tf_op jit(solution)/shard_map/reduce_scatter | solution.py:363
  620.3 18.7 %collective-permute-done.51 = f32[4,4,64,640]{3,2,1,0:T(8,128)S(1)} collective-permute-done((f32[4,4,64,640]{3,2,1,0:T(8,128)}, f32[4,4,64,640]{3,2,1,0:T(8,128)S(1)}, u32[]{:S(2)}, u32[]{:S(2)}) %collective-permute-start.51) | collective-permute-done | bytes 2621472 | tf_op jit(solution)/shard_map/ppermute | solution.py:358
  639.0 3.5 add.708
  644.2 26.8 %all_to_all.64 = f32[4,3,64,640]{3,2,1,0:T(8,128)S(1)} all-to-all(f32[4,3,64,640]{3,2,1,0:T(8,128)S(1)} %pad_maximum_fusion.14), channel_id=1, replica_groups=mesh['row'=4,'col'=4,'occ'=2] {'col'}, dimensions={0} | all-to-all | bytes 3932160 | tf_op jit(solution)/shard_map/all_to_all | solution.py:256
  671.0 32.9 %reduce-scatter.15.cloned.1.call-done = f32[1,256,640]{2,1,0:T(8,128)} async-done(((f32[4,256,640]{2,1,0:T(8,128)}), f32[1,256,640]{2,1,0:T(8,128)}) %reduce-scatter.15.cloned.1.call-update) | async-done | bytes 655376 | tf_op jit(solution)/shard_map/reduce_scatter | solution.py:363
  703.9 13.7 %all_to_all.65 = f32[4,1,64,640]{3,2,1,0:T(8,128)S(1)} all-to-all(f32[4,1,64,640]{3,2,1,0:T(8,128)} %bitcast.339), channel_id=1, replica_groups=mesh['row'=4,'col'=4,'occ'=2] {'col'}, dimensions={0} | all-to-all | bytes 1310720 | tf_op jit(solution)/shard_map/all_to_all | solution.py:256
  719.3 4.7 all-to-all-start.6
  727.3 56.2 %all-to-all-done.6 = f32[4,4,64,640]{3,2,1,0:T(8,128)} async-done(((f32[4,4,64,640]{3,2,1,0:T(8,128)}), f32[4,4,64,640]{3,2,1,0:T(8,128)}, u32[]{:S(2)}, u32[]{:S(2)}) %all-to-all-start.6) | async-done | bytes 2621472 | tf_op jit(solution)/shard_map/all_to_all | solution.py:256
  783.4 3.7 all-to-all-start.7
  801.9 16.5 %all-to-all-done.7 = f32[4,4,64,640]{3,2,1,0:T(8,128)S(1)} async-done(((f32[4,4,64,640]{3,2,1,0:T(8,128)}), f32[4,4,64,640]{3,2,1,0:T(8,128)S(1)}, u32[]{:S(2)}, u32[]{:S(2)}) %all-to-all-start.7) | async-done | bytes 2621472 | tf_op jit(solution)/shard_map/all_to_all | solution.py:256
  820.2 26.8 %shard_map.65 = f32[4,512,2,512]{3,2,1,0:T(2,128)} custom-call(s32[1]{0:T(128)} %bitcast.occ_pos_ref, s32[2,512]{1,0:T(2,128)} %constant_dynamic-slice_fusion.5.key_c_ref, s32[4,512,1]{2,1,0:T(8,128)} %copy.228.slot_r_ref, s32[4]{0:T(128)S(1)} %slice.137.irrep_i_ref, s32[512,1]{1,0:T(8,128)S(1)} %copy-done.24, s32[512,1]{1,0:T(8,128)S(1)} %copy-done.18, ...), custom_call_target="tpu_custom_call" | custom-call | flops 10737418240 | bytes 13631488 | tf_op jit(solution)/shard_map/pallas_call | solution.py:223
  (225 shorter events, 90.3 us)
Async XLA Ops:
  6.5 464.1 %reduce-scatter.9.cloned.1.call-start = ((), (), s32[]{:S(2)}) async-start(), calls=%async_computation.16 | async-start | bytes 3276800 | tf_op jit(solution)/shard_map/reduce_scatter | solution.py:363
  55.1 59.2 %collective-permute-start.25 = (f32[2,2,2,64,1024]{4,3,2,1,0:T(8,128)}, f32[2,2,2,64,1024]{4,3,2,1,0:T(8,128)}, u32[]{:S(2)}, u32[]{:S(2)}) collective-permute-start(f32[2,2,2,64,1024]{4,3,2,1,0:T(8,128)} %get-tuple-element.1186), channel_id=1, source_target_pairs={{0,2},{2,0},{4,6},{6,4},{1,3},{3,1},{5,7},{7,5},{8,10},{10,8},{12,... | collective-permute-start | bytes 6291464 | tf_op jit(solution)/shard_map/ppermute | solution.py:248
  55.6 58.8 %collective-permute-start.26 = (f32[2,2,2,64,1024]{4,3,2,1,0:T(8,128)}, f32[2,2,2,64,1024]{4,3,2,1,0:T(8,128)}, u32[]{:S(2)}, u32[]{:S(2)}) collective-permute-start(f32[2,2,2,64,1024]{4,3,2,1,0:T(8,128)} %get-tuple-element.1185), channel_id=1, source_target_pairs={{0,4},{2,6},{4,0},{6,2},{1,5},{3,7},{5,1},{7,3},{8,12},{10,14},{12... | collective-permute-start | bytes 6291464 | tf_op jit(solution)/shard_map/ppermute | solution.py:248
  58.1 91.4 %collective-permute-start.27 = (f32[2,2,2,64,1024]{4,3,2,1,0:T(8,128)}, f32[2,2,2,64,1024]{4,3,2,1,0:T(8,128)}, u32[]{:S(2)}, u32[]{:S(2)}) collective-permute-start(f32[2,2,2,64,1024]{4,3,2,1,0:T(8,128)} %get-tuple-element.1184), channel_id=1, source_target_pairs={{0,6},{2,4},{4,2},{6,0},{1,7},{3,5},{5,3},{7,1},{8,14},{10,12},{12... | collective-permute-start | bytes 6291464 | tf_op jit(solution)/shard_map/ppermute | solution.py:248
  152.7 42.2 %copy-start = (f32[4,2,2,2,64,1024]{5,4,3,2,1,0:T(8,128)}, f32[4,2,2,2,64,1024]{5,4,3,2,1,0:T(8,128)S(1)}, u32[]{:S(2)}) copy-start(f32[4,2,2,2,64,1024]{5,4,3,2,1,0:T(8,128)S(1)} %pad_maximum_fusion.7) | copy-start | bytes 25165828
  153.2 24.7 %collective-permute-start.28 = (f32[2,64,1024]{2,1,0:T(8,128)S(1)}, f32[2,64,1024]{2,1,0:T(8,128)S(1)}, u32[]{:S(2)}, u32[]{:S(2)}) collective-permute-start(f32[2,64,1024]{2,1,0:T(8,128)S(1)} %get-tuple-element.1202), channel_id=1, source_target_pairs={{0,8},{8,0},{16,24},{24,16},{1,9},{9,1},{17,25},{25,17},{2,10},{10... | collective-permute-start | bytes 1572872 | tf_op jit(solution)/shard_map/ppermute | solution.py:248
  154.8 38.2 %collective-permute-start.29 = (f32[2,64,1024]{2,1,0:T(8,128)S(1)}, f32[2,64,1024]{2,1,0:T(8,128)S(1)}, u32[]{:S(2)}, u32[]{:S(2)}) collective-permute-start(f32[2,64,1024]{2,1,0:T(8,128)S(1)} %get-tuple-element.1201), channel_id=1, source_target_pairs={{0,16},{8,24},{16,0},{24,8},{1,17},{9,25},{17,1},{25,9},{2,18},{10... | collective-permute-start | bytes 1572872 | tf_op jit(solution)/shard_map/ppermute | solution.py:248
  157.4 35.6 %collective-permute-start.30 = (f32[2,64,1024]{2,1,0:T(8,128)S(1)}, f32[2,64,1024]{2,1,0:T(8,128)S(1)}, u32[]{:S(2)}, u32[]{:S(2)}) collective-permute-start(f32[2,64,1024]{2,1,0:T(8,128)S(1)} %get-tuple-element.1200), channel_id=1, source_target_pairs={{0,24},{8,16},{16,8},{24,0},{1,25},{9,17},{17,9},{25,1},{2,26},{10... | collective-permute-start | bytes 1572872 | tf_op jit(solution)/shard_map/ppermute | solution.py:248
  193.3 51.4 %collective-permute-start.34 = (f32[1,4,2,64,1024]{4,3,2,1,0:T(8,128)S(1)}, f32[1,4,2,64,1024]{4,3,2,1,0:T(8,128)S(1)}, u32[]{:S(2)}, u32[]{:S(2)}) collective-permute-start(f32[1,4,2,64,1024]{4,3,2,1,0:T(8,128)S(1)} %maximum_bitcast_fusion.4), channel_id=1, source_target_pairs={{0,4},{2,6},{4,0},{6,2},{1,5},{3,7},{5,1},{7,3},{8,12},{10,14},{12... | collective-permute-start | bytes 6291464 | tf_op jit(solution)/shard_map/ppermute | solution.py:248
  195.4 31.7 %collective-permute-start.31 = (f32[2,64,1024]{2,1,0:T(8,128)S(1)}, f32[2,64,1024]{2,1,0:T(8,128)S(1)}, u32[]{:S(2)}, u32[]{:S(2)}) collective-permute-start(f32[2,64,1024]{2,1,0:T(8,128)S(1)} %get-tuple-element.1198), channel_id=1, source_target_pairs={{0,8},{8,0},{16,24},{24,16},{1,9},{9,1},{17,25},{25,17},{2,10},{10... | collective-permute-start | bytes 1572872 | tf_op jit(solution)/shard_map/ppermute | solution.py:248
  206.2 38.2 %collective-permute-start.32 = (f32[2,64,1024]{2,1,0:T(8,128)S(1)}, f32[2,64,1024]{2,1,0:T(8,128)S(1)}, u32[]{:S(2)}, u32[]{:S(2)}) collective-permute-start(f32[2,64,1024]{2,1,0:T(8,128)S(1)} %get-tuple-element.1197), channel_id=1, source_target_pairs={{0,16},{8,24},{16,0},{24,8},{1,17},{9,25},{17,1},{25,9},{2,18},{10... | collective-permute-start | bytes 1572872 | tf_op jit(solution)/shard_map/ppermute | solution.py:248
  207.3 37.1 %collective-permute-start.33 = (f32[2,64,1024]{2,1,0:T(8,128)S(1)}, f32[2,64,1024]{2,1,0:T(8,128)S(1)}, u32[]{:S(2)}, u32[]{:S(2)}) collective-permute-start(f32[2,64,1024]{2,1,0:T(8,128)S(1)} %get-tuple-element.1196), channel_id=1, source_target_pairs={{0,24},{8,16},{16,8},{24,0},{1,25},{9,17},{17,9},{25,1},{2,26},{10... | collective-permute-start | bytes 1572872 | tf_op jit(solution)/shard_map/ppermute | solution.py:248
  247.0 7.5 collective-permute-start.39
  250.8 76.3 %collective-permute-start.38 = (f32[1,4,2,64,1024]{4,3,2,1,0:T(8,128)S(1)}, f32[1,4,2,64,1024]{4,3,2,1,0:T(8,128)}, u32[]{:S(2)}, u32[]{:S(2)}) collective-permute-start(f32[1,4,2,64,1024]{4,3,2,1,0:T(8,128)S(1)} %maximum_bitcast_fusion.5), channel_id=1, source_target_pairs={{0,4},{2,6},{4,0},{6,2},{1,5},{3,7},{5,1},{7,3},{8,12},{10,14},{12... | collective-permute-start | bytes 6291464 | tf_op jit(solution)/shard_map/ppermute | solution.py:248
  271.9 76.7 %collective-permute-start.40 = (f32[4,4,64,640]{3,2,1,0:T(8,128)}, f32[4,4,64,640]{3,2,1,0:T(8,128)}, u32[]{:S(2)}, u32[]{:S(2)}) collective-permute-start(f32[4,4,64,640]{3,2,1,0:T(8,128)} %shard_map.57), channel_id=1, source_target_pairs={{0,1},{1,0},{2,3},{3,2},{4,5},{5,4},{6,7},{7,6},{8,9},{9,8},{10,11... | collective-permute-start | bytes 7864328 | tf_op jit(solution)/shard_map/ppermute | solution.py:358
  276.3 32.1 %collective-permute-start.35 = (f32[2,64,1024]{2,1,0:T(8,128)}, f32[2,64,1024]{2,1,0:T(8,128)}, u32[]{:S(2)}, u32[]{:S(2)}) collective-permute-start(f32[2,64,1024]{2,1,0:T(8,128)} %get-tuple-element.1194), channel_id=1, source_target_pairs={{0,8},{8,0},{16,24},{24,16},{1,9},{9,1},{17,25},{25,17},{2,10},{10... | collective-permute-start | bytes 1572872 | tf_op jit(solution)/shard_map/ppermute | solution.py:248
  285.7 38.5 %collective-permute-start.36 = (f32[2,64,1024]{2,1,0:T(8,128)}, f32[2,64,1024]{2,1,0:T(8,128)}, u32[]{:S(2)}, u32[]{:S(2)}) collective-permute-start(f32[2,64,1024]{2,1,0:T(8,128)} %get-tuple-element.1193), channel_id=1, source_target_pairs={{0,16},{8,24},{16,0},{24,8},{1,17},{9,25},{17,1},{25,9},{2,18},{10... | collective-permute-start | bytes 1572872 | tf_op jit(solution)/shard_map/ppermute | solution.py:248
  286.7 37.5 %collective-permute-start.37 = (f32[2,64,1024]{2,1,0:T(8,128)S(1)}, f32[2,64,1024]{2,1,0:T(8,128)}, u32[]{:S(2)}, u32[]{:S(2)}) collective-permute-start(f32[2,64,1024]{2,1,0:T(8,128)S(1)} %get-tuple-element.1192), channel_id=1, source_target_pairs={{0,24},{8,16},{16,8},{24,0},{1,25},{9,17},{17,9},{25,1},{2,26},{10... | collective-permute-start | bytes 1572872 | tf_op jit(solution)/shard_map/ppermute | solution.py:248
  288.9 42.3 %copy-start.41 = (s32[20]{0:T(128)}, s32[20]{0:T(128)S(1)}, u32[]{:S(2)}) copy-start(s32[20]{0:T(128)S(1)} %concatenate.121.scalar_ref) | copy-start | bytes 244
  348.6 7.5 collective-permute-start.45
  352.9 193.4 %reduce-scatter.11.cloned.1.call-start = ((), (), s32[]{:S(2)}) async-start(), calls=%async_computation.17 | async-start | bytes 3276800 | tf_op jit(solution)/shard_map/reduce_scatter | solution.py:363
  354.9 94.5 %collective-permute-start.44 = (f32[1,4,2,64,1024]{4,3,2,1,0:T(8,128)S(1)}, f32[1,4,2,64,1024]{4,3,2,1,0:T(8,128)}, u32[]{:S(2)}, u32[]{:S(2)}) collective-permute-start(f32[1,4,2,64,1024]{4,3,2,1,0:T(8,128)S(1)} %copy-done.7), channel_id=1, source_target_pairs={{0,4},{2,6},{4,0},{6,2},{1,5},{3,7},{5,1},{7,3},{8,12},{10,14},{12... | collective-permute-start | bytes 6291464 | tf_op jit(solution)/shard_map/ppermute | solution.py:248
  373.9 96.8 %collective-permute-start.46 = (f32[4,4,64,640]{3,2,1,0:T(8,128)}, f32[4,4,64,640]{3,2,1,0:T(8,128)}, u32[]{:S(2)}, u32[]{:S(2)}) collective-permute-start(f32[4,4,64,640]{3,2,1,0:T(8,128)} %shard_map.59), channel_id=1, source_target_pairs={{0,1},{1,0},{2,3},{3,2},{4,5},{5,4},{6,7},{7,6},{8,9},{9,8},{10,11... | collective-permute-start | bytes 7864328 | tf_op jit(solution)/shard_map/ppermute | solution.py:358
  377.4 55.7 %collective-permute-start.41 = (f32[2,64,1024]{2,1,0:T(8,128)}, f32[2,64,1024]{2,1,0:T(8,128)}, u32[]{:S(2)}, u32[]{:S(2)}) collective-permute-start(f32[2,64,1024]{2,1,0:T(8,128)} %get-tuple-element.1190), channel_id=1, source_target_pairs={{0,8},{8,0},{16,24},{24,16},{1,9},{9,1},{17,25},{25,17},{2,10},{10... | collective-permute-start | bytes 1572872 | tf_op jit(solution)/shard_map/ppermute | solution.py:248
  388.3 44.8 %collective-permute-start.42 = (f32[2,64,1024]{2,1,0:T(8,128)}, f32[2,64,1024]{2,1,0:T(8,128)}, u32[]{:S(2)}, u32[]{:S(2)}) collective-permute-start(f32[2,64,1024]{2,1,0:T(8,128)} %get-tuple-element.1189), channel_id=1, source_target_pairs={{0,16},{8,24},{16,0},{24,8},{1,17},{9,25},{17,1},{25,9},{2,18},{10... | collective-permute-start | bytes 1572872 | tf_op jit(solution)/shard_map/ppermute | solution.py:248
  389.3 57.2 %collective-permute-start.43 = (f32[2,64,1024]{2,1,0:T(8,128)S(1)}, f32[2,64,1024]{2,1,0:T(8,128)}, u32[]{:S(2)}, u32[]{:S(2)}) collective-permute-start(f32[2,64,1024]{2,1,0:T(8,128)S(1)} %get-tuple-element.1188), channel_id=1, source_target_pairs={{0,24},{8,16},{16,8},{24,0},{1,25},{9,17},{17,9},{25,1},{2,26},{10... | collective-permute-start | bytes 1572872 | tf_op jit(solution)/shard_map/ppermute | solution.py:248
  391.5 61.9 %copy-start.45 = (s32[20]{0:T(128)}, s32[20]{0:T(128)S(1)}, u32[]{:S(2)}) copy-start(s32[20]{0:T(128)S(1)} %concatenate.124.scalar_ref) | copy-start | bytes 244
  470.7 7.6 collective-permute-start.48
  475.1 145.2 %reduce-scatter.13.cloned.1.call-start = ((), (), s32[]{:S(2)}) async-start(), calls=%async_computation.18 | async-start | bytes 3276800 | tf_op jit(solution)/shard_map/reduce_scatter | solution.py:363
  476.7 48.1 %collective-permute-start.47 = (f32[1,4,2,64,1024]{4,3,2,1,0:T(8,128)S(1)}, f32[1,4,2,64,1024]{4,3,2,1,0:T(8,128)}, u32[]{:S(2)}, u32[]{:S(2)}) collective-permute-start(f32[1,4,2,64,1024]{4,3,2,1,0:T(8,128)S(1)} %copy-done.8), channel_id=1, source_target_pairs={{0,4},{2,6},{4,0},{6,2},{1,5},{3,7},{5,1},{7,3},{8,12},{10,14},{12... | collective-permute-start | bytes 6291464 | tf_op jit(solution)/shard_map/ppermute | solution.py:248
  495.6 59.2 %collective-permute-start.49 = (f32[4,4,64,640]{3,2,1,0:T(8,128)}, f32[4,4,64,640]{3,2,1,0:T(8,128)}, u32[]{:S(2)}, u32[]{:S(2)}) collective-permute-start(f32[4,4,64,640]{3,2,1,0:T(8,128)} %shard_map.61), channel_id=1, source_target_pairs={{0,1},{1,0},{2,3},{3,2},{4,5},{5,4},{6,7},{7,6},{8,9},{9,8},{10,11... | collective-permute-start | bytes 7864328 | tf_op jit(solution)/shard_map/ppermute | solution.py:358
  497.7 31.1 %copy-start.49 = (s32[20]{0:T(128)}, s32[20]{0:T(128)S(1)}, u32[]{:S(2)}) copy-start(s32[20]{0:T(128)S(1)} %concatenate.127.scalar_ref) | copy-start | bytes 244
  554.8 7.5 collective-permute-start.50
  559.2 144.8 %reduce-scatter.15.cloned.1.call-start = ((), (), s32[]{:S(2)}) async-start(), calls=%async_computation.19 | async-start | bytes 3276800 | tf_op jit(solution)/shard_map/reduce_scatter | solution.py:363
  579.9 59.1 %collective-permute-start.51 = (f32[4,4,64,640]{3,2,1,0:T(8,128)}, f32[4,4,64,640]{3,2,1,0:T(8,128)S(1)}, u32[]{:S(2)}, u32[]{:S(2)}) collective-permute-start(f32[4,4,64,640]{3,2,1,0:T(8,128)} %shard_map.63), channel_id=1, source_target_pairs={{0,1},{1,0},{2,3},{3,2},{4,5},{5,4},{6,7},{7,6},{8,9},{9,8},{10,11... | collective-permute-start | bytes 7864328 | tf_op jit(solution)/shard_map/ppermute | solution.py:358
  719.3 64.1 %all-to-all-start.6 = ((f32[4,4,64,640]{3,2,1,0:T(8,128)}), f32[4,4,64,640]{3,2,1,0:T(8,128)}, u32[]{:S(2)}, u32[]{:S(2)}) async-start(f32[4,4,64,640]{3,2,1,0:T(8,128)} %pad_maximum_fusion.13), calls=%async_computation.14 | async-start | bytes 5242880 | tf_op jit(solution)/shard_map/all_to_all | solution.py:256
  725.7 61.5 %copy-start.29 = (s32[4,4]{1,0:T(4,128)S(1)}, s32[4,4]{1,0:T(4,128)}, u32[]{:S(2)}) copy-start(s32[4,4]{1,0:T(4,128)} %copy-done.28) | copy-start | bytes 196
  725.7 67.6 %copy-start.32 = (s32[512]{0:T(512)S(1)}, s32[512]{0:T(512)}, u32[]{:S(2)}) copy-start(s32[512]{0:T(512)} %copy-done.31) | copy-start | bytes 6148
  725.7 67.7 %copy-start.35 = (s32[1,512]{1,0:T(1,128)S(1)}, s32[1,512]{1,0:T(1,128)}, u32[]{:S(2)}) copy-start(s32[1,512]{1,0:T(1,128)} %get-tuple-element.1218) | copy-start | bytes 6148
  725.7 67.7 %copy-start.36 = (s32[1,512]{1,0:T(1,128)S(1)}, s32[1,512]{1,0:T(1,128)}, u32[]{:S(2)}) copy-start(s32[1,512]{1,0:T(1,128)} %get-tuple-element.1219) | copy-start | bytes 6148
  725.7 67.7 %copy-start.37 = (s32[1,512]{1,0:T(1,128)S(1)}, s32[1,512]{1,0:T(1,128)}, u32[]{:S(2)}) copy-start(s32[1,512]{1,0:T(1,128)} %get-tuple-element.1220) | copy-start | bytes 6148
  725.7 69.0 %copy-start.34 = (s32[1,512]{1,0:T(1,128)S(1)}, s32[1,512]{1,0:T(1,128)}, u32[]{:S(2)}) copy-start(s32[1,512]{1,0:T(1,128)} %get-tuple-element.1162) | copy-start | bytes 6148
  725.7 69.5 %copy-start.33 = (s32[512,1]{0,1:T(1,128)S(1)}, s32[512,1]{0,1:T(1,128)}, u32[]{:S(2)}) copy-start(s32[512,1]{0,1:T(1,128)} %get-tuple-element.1163) | copy-start | bytes 6148
  725.7 94.3 %collective-permute-start.52 = (f32[2,512,640]{2,1,0:T(8,128)}, f32[2,512,640]{2,1,0:T(8,128)}, u32[]{:S(2)}, u32[]{:S(2)}) collective-permute-start(f32[2,512,640]{2,1,0:T(8,128)} %bitcast.96.own_ref), channel_id=1, source_target_pairs={{0,1},{1,0},{2,3},{3,2},{4,5},{5,4},{6,7},{7,6},{8,9},{9,8},{10,11... | collective-permute-start | bytes 7864328 | tf_op jit(solution)/shard_map/ppermute | solution.py:373
  783.4 34.9 %all-to-all-start.7 = ((f32[4,4,64,640]{3,2,1,0:T(8,128)}), f32[4,4,64,640]{3,2,1,0:T(8,128)S(1)}, u32[]{:S(2)}, u32[]{:S(2)}) async-start(f32[4,4,64,640]{3,2,1,0:T(8,128)} %all-to-all-done.6), calls=%async_computation.15 | async-start | bytes 5242880 | tf_op jit(solution)/shard_map/all_to_all | solution.py:256
  820.1 26.9 %copy-start.15 = (s32[4,2,4,64,1]{3,2,0,4,1:T(4,128)S(1)}, s32[4,2,4,64,1]{3,2,0,4,1:T(4,128)}, u32[]{:S(2)}) copy-start(s32[4,2,4,64,1]{3,2,0,4,1:T(4,128)} %copy-done.14) | copy-start | bytes 24580
  820.1 26.9 %copy-start.40 = (s32[20]{0:T(128)S(1)}, s32[20]{0:T(128)}, u32[]{:S(2)}) copy-start(s32[20]{0:T(128)} %copy-done.39) | copy-start | bytes 244
  820.1 26.9 %copy-start.42 = (s32[20]{0:T(128)S(1)}, s32[20]{0:T(128)}, u32[]{:S(2)}) copy-start(s32[20]{0:T(128)} %copy-done.41) | copy-start | bytes 244
  (28 other events, 341.5 us)
Sparse Core Ops, SparseCore 0:
  353.1 79.9 reduce-scatter.8
  475.3 60.3 reduce-scatter.10
  559.3 60.9 reduce-scatter.12
  642.7 61.1 reduce-scatter.14

commit v3 on v2

--- a/solution.py
+++ b/solution.py
@@ -203,7 +203,7 @@
 
 def finish(tables, own, swapped, turned, base, cap, shape):
     n_i, tile_a, half, tile_b = shape
-    rows = min(tile_a, 256)
+    rows = min(tile_a, 512)
     block = pl.BlockSpec((1, rows, half, tile_b), lambda i, s: (i, s, 0, 0))
     part = pl.BlockSpec((1, tile_a, cap), lambda i, s: (i % half, 0, 0))
     smem = pl.BlockSpec(memory_space=pltpu.SMEM)
@@ -344,10 +344,11 @@
         live = {"spread": spread, "right": (right_high, right_low)}
         for step in range(len(every) + 3):
             new = dict(live)
-            for stage in range(4):
+            for stage in range(5):
                 k = step - stage
                 if not 0 <= k < len(every):
                     continue
+                wait = int(k == 0 and len(every) > 2)
                 if stage == 0:
                     new["near", k] = to_plane(live["spread"], k)
                 elif stage == 1:
@@ -356,9 +357,15 @@
                 elif stage == 2:
                     left_rows = live["full", k], flipped(live["full", k], "col", n, 1)
                     new["got", k] = lax.ppermute(multiply(k, *left_rows, live["right"], 1 - occ_pos), "occ", swap)
-                    new["kept", k] = multiply(k, *left_rows, live["right"], occ_pos)
+                    if wait:
+                        new["rows", k] = left_rows
+                    else:
+                        new["kept", k] = multiply(k, *left_rows, live["right"], occ_pos)
                     del new["full", k]
-                else:
+                elif stage == 3 and wait:
+                    new["kept", k] = multiply(k, *live["rows", k], live["right"], occ_pos)
+                    del new["rows", k]
+                elif stage == 3 + wait:
                     total = (live["kept", k] + live["got", k]).reshape(n, n * sub, cap)
                     new["part", k] = lax.psum_scatter(total, "row", scatter_dimension=0, tiled=True)[0]
                     del new["kept", k], new["got", k]

time: 864 us -> 846 us (0.979)
    ppermute x23, waiting for transfers between devices: 230 us -> 201 us  [flipped(): return lax.ppermute(x, axis, [(d, d ^ bits) for d in range(n)])]
    reduce_scatter x4, waiting for transfers between devices: 53.8 us -> 73.5 us  [one_round(): lax.psum_scatter(total, 'row', scatter_dimension=0, tiled=True)[0]]
  transfers between devices with their start and end apart: 34 -> 34, of which waited for: 20 -> 21; matrix products, arithmetic and copies ran while one was open for 10% -> 9% of each run, Pallas kernels for 21% -> 19%
where the time goes in v3:
time: 846 us; the launch traced here: 839 us
  waiting for transfers between devices  379 us (45%)
  Pallas kernels  212 us (25%)
  local copies, waits for them, and re-layouts  64.5 us (8%)
  starting transfers between devices  63.2 us (7%)
  other arithmetic  57.3 us (7%)
  blocking collectives  40.6 us (5%)
  between operations  22.1 us (3%)
    ppermute x23, waiting for transfers between devices, flipped(): return lax.ppermute(x, axis, [(d, d ^ bits) for d in range(n)])  201 us
    pallas_call x8, Pallas kernels, product(): pl.pallas_call(functools.partial(product_body, cap), out_shape=jax.ShapeD...  140 us
    reduce_scatter x4, waiting for transfers between devices, one_round(): lax.psum_scatter(total, 'row', scatter_dimension=0, tiled=True)[0]  73.5 us
    all_to_all x2, waiting for transfers between devices, spread_out(): return lax.all_to_all(x, axis, split_axis=0, concat_axis=0, tiled=True)  72.6 us
    ppermute x23, starting transfers between devices, flipped(): return lax.ppermute(x, axis, [(d, d ^ bits) for d in range(n)])  47.9 us
    all_to_all x2, blocking collectives, spread_out(): return lax.all_to_all(x, axis, split_axis=0, concat_axis=0, tiled=True)  40.6 us
    pallas_call x1, Pallas kernels, compact(): pl.pallas_call(functools.partial(compact_body, cap), out_shape=(out, out)...  36.4 us
    ppermute x4, waiting for transfers between devices, one_round(): lax.ppermute(multiply(k, *left_rows, live['right'], 1 - occ_pos), 'occ',...  31.9 us
  transfers between devices with their start and end apart: 34, of which 21 were waited for; matrix products, arithmetic and copies ran while one was open for 9% of the time, Pallas kernels for 19%

profile of v3, /device:TPU:0, one launch (start us, length us, event | category | flops | bytes accessed | tf_op | source)
XLA Modules:
  0.0 839.1 jit_solution(3869453055716731347)
XLA Ops:
  17.2 3.1 fusion.59
  21.7 11.8 %reshape.810.rows_ref = f32[4,512,1024]{2,1,0:T(8,128)} reshape(f32[4,512,2,512]{3,2,1,0:T(2,128)} %param.7) | data formatting | bytes 16777216 | tf_op jit(solution)/shard_map/reshape | solution.py:51
  33.5 5.5 fusion.68
  39.0 9.4 %shard_map.55 = f32[2,2,4,2,64,1024]{5,4,3,2,1,0:T(8,128)} custom-call(s32[1,512]{1,0:T(1,128)} %get-tuple-element.1171.place_ref, f32[4,512,1024]{2,1,0:T(8,128)} %reshape.810.rows_ref), custom_call_target="tpu_custom_call" | custom-call | flops 4294967296 | bytes 16777216 | tf_op jit(solution)/shard_map/pallas_call | solution.py:38
  48.4 6.8 dynamic-slice_bitcast_fusion.19
  66.9 10.9 %copy.240 = f32[128,8,4,512]{3,1,2,0:T(8,128)} copy(f32[128,8,4,512]{3,2,1,0:T(4,128)} %bitcast.304) | data formatting | bytes 16777216
  77.8 36.4 %shard_map.56 = (bf16[1024,2560]{1,0:T(8,128)(2,1)}, bf16[1024,2560]{1,0:T(8,128)(2,1)}) custom-call(s32[4,512,1]{2,1,0:T(8,128)} %and_select_fusion.key_ref, f32[1024,2048]{1,0:T(8,128)} %bitcast.335), custom_call_target="tpu_custom_call" | custom-call | flops 21474836480 | bytes 8388608 | tf_op jit(solution)/shard_map/pallas_call | solution.py:85
  114.2 35.3 %collective-permute-done.27 = f32[2,2,2,64,1024]{4,3,2,1,0:T(8,128)} collective-permute-done((f32[2,2,2,64,1024]{4,3,2,1,0:T(8,128)}, f32[2,2,2,64,1024]{4,3,2,1,0:T(8,128)}, u32[]{:S(2)}, u32[]{:S(2)}) %collective-permute-start.27) | collective-permute-done | bytes 2097184 | tf_op jit(solution)/shard_map/ppermute | solution.py:248
  149.6 3.2 pad_maximum_fusion.7
  157.7 20.2 %collective-permute-done.28 = f32[2,64,1024]{2,1,0:T(8,128)S(1)} collective-permute-done((f32[2,64,1024]{2,1,0:T(8,128)S(1)}, f32[2,64,1024]{2,1,0:T(8,128)S(1)}, u32[]{:S(2)}, u32[]{:S(2)}) %collective-permute-start.28) | collective-permute-done | bytes 524320 | tf_op jit(solution)/shard_map/ppermute | solution.py:248
  178.0 15.1 %collective-permute-done.29 = f32[2,64,1024]{2,1,0:T(8,128)S(1)} collective-permute-done((f32[2,64,1024]{2,1,0:T(8,128)S(1)}, f32[2,64,1024]{2,1,0:T(8,128)S(1)}, u32[]{:S(2)}, u32[]{:S(2)}) %collective-permute-start.29) | collective-permute-done | bytes 524320 | tf_op jit(solution)/shard_map/ppermute | solution.py:248
  195.4 10.9 %collective-permute-start.31 = (f32[2,64,1024]{2,1,0:T(8,128)S(1)}, f32[2,64,1024]{2,1,0:T(8,128)S(1)}, u32[]{:S(2)}, u32[]{:S(2)}) collective-permute-start(f32[2,64,1024]{2,1,0:T(8,128)S(1)} %get-tuple-element.1208), channel_id=1, source_target_pairs={{0,8},{8,0},{16,24},{24,16},{1,9},{9,1},{17,25},{25,17},{2,10},{10... | collective-permute-start | bytes 1572872 | tf_op jit(solution)/shard_map/ppermute | solution.py:248
  208.8 18.4 %collective-permute-done.31 = f32[2,64,1024]{2,1,0:T(8,128)S(1)} collective-permute-done((f32[2,64,1024]{2,1,0:T(8,128)S(1)}, f32[2,64,1024]{2,1,0:T(8,128)S(1)}, u32[]{:S(2)}, u32[]{:S(2)}) %collective-permute-start.31) | collective-permute-done | bytes 524320 | tf_op jit(solution)/shard_map/ppermute | solution.py:248
  227.2 17.4 %collective-permute-done.32 = f32[2,64,1024]{2,1,0:T(8,128)S(1)} collective-permute-done((f32[2,64,1024]{2,1,0:T(8,128)S(1)}, f32[2,64,1024]{2,1,0:T(8,128)S(1)}, u32[]{:S(2)}, u32[]{:S(2)}) %collective-permute-start.32) | collective-permute-done | bytes 524320 | tf_op jit(solution)/shard_map/ppermute | solution.py:248
  250.9 3.7 collective-permute-done.39.far_ref
  254.6 17.3 %shard_map.57 = f32[4,4,64,640]{3,2,1,0:T(8,128)} custom-call(s32[20]{0:T(128)S(1)} %concatenate.120.scalar_ref, s32[4,4,64,1]{3,2,1,0:T(8,128)} %copy.219.irrep_ref, f32[2,4,2,64,1024]{4,3,2,1,0:T(8,128)} %pad_maximum_fusion.8.near_ref, f32[2,4,2,64,1024]{4,3,2,1,0:T(8,128)} %collective-permute-done.39.far_ref, ...), custom_call_target="tpu_custom_call" | custom-call | flops 8053063680 | bytes 14680064 | tf_op jit(solution)/shard_map/pallas_call | solution.py:147
  276.0 9.4 %collective-permute-start.35 = (f32[2,64,1024]{2,1,0:T(8,128)S(1)}, f32[2,64,1024]{2,1,0:T(8,128)S(1)}, u32[]{:S(2)}, u32[]{:S(2)}) collective-permute-start(f32[2,64,1024]{2,1,0:T(8,128)S(1)} %get-tuple-element.1204), channel_id=1, source_target_pairs={{0,8},{8,0},{16,24},{24,16},{1,9},{9,1},{17,25},{25,17},{2,10},{10... | collective-permute-start | bytes 1572872 | tf_op jit(solution)/shard_map/ppermute | solution.py:248
  287.9 19.5 %collective-permute-done.35 = f32[2,64,1024]{2,1,0:T(8,128)S(1)} collective-permute-done((f32[2,64,1024]{2,1,0:T(8,128)S(1)}, f32[2,64,1024]{2,1,0:T(8,128)S(1)}, u32[]{:S(2)}, u32[]{:S(2)}) %collective-permute-start.35) | collective-permute-done | bytes 524320 | tf_op jit(solution)/shard_map/ppermute | solution.py:248
  307.4 16.2 %collective-permute-done.36 = f32[2,64,1024]{2,1,0:T(8,128)S(1)} collective-permute-done((f32[2,64,1024]{2,1,0:T(8,128)S(1)}, f32[2,64,1024]{2,1,0:T(8,128)S(1)}, u32[]{:S(2)}, u32[]{:S(2)}) %collective-permute-start.36) | collective-permute-done | bytes 524320 | tf_op jit(solution)/shard_map/ppermute | solution.py:248
  327.4 3.7 collective-permute-done.40
  333.5 5.1 collective-permute-done.45.far_ref
  338.6 17.9 %shard_map.58 = f32[4,4,64,640]{3,2,1,0:T(8,128)} custom-call(s32[20]{0:T(128)S(1)} %concatenate.122.scalar_ref, s32[4,4,64,1]{3,2,1,0:T(8,128)} %copy.220.irrep_ref, f32[2,4,2,64,1024]{4,3,2,1,0:T(8,128)} %pad_maximum_fusion.9.near_ref, f32[2,4,2,64,1024]{4,3,2,1,0:T(8,128)} %collective-permute-done.45.far_ref, ...), custom_call_target="tpu_custom_call" | custom-call | flops 8053063680 | bytes 14680064 | tf_op jit(solution)/shard_map/pallas_call | solution.py:147
  361.2 9.4 %collective-permute-start.41 = (f32[2,64,1024]{2,1,0:T(8,128)S(1)}, f32[2,64,1024]{2,1,0:T(8,128)S(1)}, u32[]{:S(2)}, u32[]{:S(2)}) collective-permute-start(f32[2,64,1024]{2,1,0:T(8,128)S(1)} %get-tuple-element.1200), channel_id=1, source_target_pairs={{0,8},{8,0},{16,24},{24,16},{1,9},{9,1},{17,25},{25,17},{2,10},{10... | collective-permute-start | bytes 1572872 | tf_op jit(solution)/shard_map/ppermute | solution.py:248
  373.2 17.4 %shard_map.60 = f32[4,4,64,640]{3,2,1,0:T(8,128)} custom-call(s32[20]{0:T(128)S(1)} %concatenate.124.scalar_ref, s32[4,4,64,1]{3,2,1,0:T(8,128)} %copy.219.irrep_ref, f32[2,4,2,64,1024]{4,3,2,1,0:T(8,128)} %pad_maximum_fusion.8.near_ref, f32[2,4,2,64,1024]{4,3,2,1,0:T(8,128)} %collective-permute-done.39.far_ref, ...), custom_call_target="tpu_custom_call" | custom-call | flops 8053063680 | bytes 14680064 | tf_op jit(solution)/shard_map/pallas_call | solution.py:147
  393.1 15.8 %collective-permute-done.42 = f32[2,64,1024]{2,1,0:T(8,128)S(1)} collective-permute-done((f32[2,64,1024]{2,1,0:T(8,128)S(1)}, f32[2,64,1024]{2,1,0:T(8,128)S(1)}, u32[]{:S(2)}, u32[]{:S(2)}) %collective-permute-start.42) | collective-permute-done | bytes 524320 | tf_op jit(solution)/shard_map/ppermute | solution.py:248
  410.5 4.0 pad_maximum_fusion.10.near_ref
  414.5 17.5 %shard_map.59 = f32[4,4,64,640]{3,2,1,0:T(8,128)} custom-call(s32[20]{0:T(128)S(1)} %concatenate.123.scalar_ref, s32[4,4,64,1]{3,2,1,0:T(8,128)} %copy.220.irrep_ref, f32[2,4,2,64,1024]{4,3,2,1,0:T(8,128)} %pad_maximum_fusion.9.near_ref, f32[2,4,2,64,1024]{4,3,2,1,0:T(8,128)} %collective-permute-done.45.far_ref, ...), custom_call_target="tpu_custom_call" | custom-call | flops 8053063680 | bytes 14680064 | tf_op jit(solution)/shard_map/pallas_call | solution.py:147
  432.0 3.6 add.706
  435.7 4.3 add.705
  443.2 17.4 %shard_map.61 = f32[4,4,64,640]{3,2,1,0:T(8,128)} custom-call(s32[20]{0:T(128)S(1)} %concatenate.126.scalar_ref, s32[4,4,64,1]{3,2,1,0:T(8,128)} %copy.219.irrep_ref, f32[2,4,2,64,1024]{4,3,2,1,0:T(8,128)} %pad_maximum_fusion.10.near_ref, f32[2,4,2,64,1024]{4,3,2,1,0:T(8,128)} %collective-permute-done.48.far_ref, ...), custom_call_target="tpu_custom_call" | custom-call | flops 8053063680 | bytes 14680064 | tf_op jit(solution)/shard_map/pallas_call | solution.py:147
  462.0 27.1 %collective-permute-done.47 = f32[1,4,2,64,1024]{4,3,2,1,0:T(8,128)} collective-permute-done((f32[1,4,2,64,1024]{4,3,2,1,0:T(8,128)S(1)}, f32[1,4,2,64,1024]{4,3,2,1,0:T(8,128)}, u32[]{:S(2)}, u32[]{:S(2)}) %collective-permute-start.47) | collective-permute-done | bytes 2097184 | tf_op jit(solution)/shard_map/ppermute | solution.py:248
  489.0 4.0 pad_maximum_fusion.11.near_ref
  493.1 17.4 %shard_map.62 = f32[4,4,64,640]{3,2,1,0:T(8,128)} custom-call(s32[20]{0:T(128)S(1)} %concatenate.127.scalar_ref, s32[4,4,64,1]{3,2,1,0:T(8,128)} %copy.219.irrep_ref, f32[2,4,2,64,1024]{4,3,2,1,0:T(8,128)} %pad_maximum_fusion.10.near_ref, f32[2,4,2,64,1024]{4,3,2,1,0:T(8,128)} %collective-permute-done.48.far_ref, ...), custom_call_target="tpu_custom_call" | custom-call | flops 8053063680 | bytes 14680064 | tf_op jit(solution)/shard_map/pallas_call | solution.py:147
  510.5 38.7 %reduce-scatter.9.cloned.1.call-done = f32[1,256,640]{2,1,0:T(8,128)} async-done(((f32[4,256,640]{2,1,0:T(8,128)}), f32[1,256,640]{2,1,0:T(8,128)}) %reduce-scatter.9.cloned.1.call-update) | async-done | bytes 655376 | tf_op jit(solution)/shard_map/reduce_scatter | solution.py:370
  549.2 4.3 add.707
  556.7 18.0 %shard_map.63 = f32[4,4,64,640]{3,2,1,0:T(8,128)} custom-call(s32[20]{0:T(128)S(1)} %concatenate.128.scalar_ref, s32[4,4,64,1]{3,2,1,0:T(8,128)} %copy.220.irrep_ref, f32[2,4,2,64,1024]{4,3,2,1,0:T(8,128)} %pad_maximum_fusion.11.near_ref, f32[2,4,2,64,1024]{4,3,2,1,0:T(8,128)} %collective-permute-done.50.far_ref, ...), custom_call_target="tpu_custom_call" | custom-call | flops 8053063680 | bytes 14680064 | tf_op jit(solution)/shard_map/pallas_call | solution.py:147
  576.9 17.4 %shard_map.64 = f32[4,4,64,640]{3,2,1,0:T(8,128)} custom-call(s32[20]{0:T(128)S(1)} %concatenate.129.scalar_ref, s32[4,4,64,1]{3,2,1,0:T(8,128)} %copy.220.irrep_ref, f32[2,4,2,64,1024]{4,3,2,1,0:T(8,128)} %pad_maximum_fusion.11.near_ref, f32[2,4,2,64,1024]{4,3,2,1,0:T(8,128)} %collective-permute-done.50.far_ref, ...), custom_call_target="tpu_custom_call" | custom-call | flops 8053063680 | bytes 14680064 | tf_op jit(solution)/shard_map/pallas_call | solution.py:147
  594.3 11.3 %reduce-scatter.13.cloned.1.call-done = f32[1,256,640]{2,1,0:T(8,128)} async-done(((f32[4,256,640]{2,1,0:T(8,128)}), f32[1,256,640]{2,1,0:T(8,128)}) %reduce-scatter.13.cloned.1.call-update) | async-done | bytes 655376 | tf_op jit(solution)/shard_map/reduce_scatter | solution.py:370
  605.7 28.2 %collective-permute-done.51 = f32[4,4,64,640]{3,2,1,0:T(8,128)S(1)} collective-permute-done((f32[4,4,64,640]{3,2,1,0:T(8,128)}, f32[4,4,64,640]{3,2,1,0:T(8,128)S(1)}, u32[]{:S(2)}, u32[]{:S(2)}) %collective-permute-start.51) | collective-permute-done | bytes 2621472 | tf_op jit(solution)/shard_map/ppermute | solution.py:359
  633.8 3.5 add.708
  639.0 26.9 %all_to_all.64 = f32[4,3,64,640]{3,2,1,0:T(8,128)S(1)} all-to-all(f32[4,3,64,640]{3,2,1,0:T(8,128)S(1)} %pad_maximum_fusion.14), channel_id=1, replica_groups=mesh['row'=4,'col'=4,'occ'=2] {'col'}, dimensions={0} | all-to-all | bytes 3932160 | tf_op jit(solution)/shard_map/all_to_all | solution.py:256
  665.8 23.5 %reduce-scatter.15.cloned.1.call-done = f32[1,256,640]{2,1,0:T(8,128)} async-done(((f32[4,256,640]{2,1,0:T(8,128)}), f32[1,256,640]{2,1,0:T(8,128)}) %reduce-scatter.15.cloned.1.call-update) | async-done | bytes 655376 | tf_op jit(solution)/shard_map/reduce_scatter | solution.py:370
  689.3 13.7 %all_to_all.65 = f32[4,1,64,640]{3,2,1,0:T(8,128)S(1)} all-to-all(f32[4,1,64,640]{3,2,1,0:T(8,128)} %bitcast.336), channel_id=1, replica_groups=mesh['row'=4,'col'=4,'occ'=2] {'col'}, dimensions={0} | all-to-all | bytes 1310720 | tf_op jit(solution)/shard_map/all_to_all | solution.py:256
  704.7 4.7 all-to-all-start.6
  712.7 56.2 %all-to-all-done.6 = f32[4,4,64,640]{3,2,1,0:T(8,128)} async-done(((f32[4,4,64,640]{3,2,1,0:T(8,128)}), f32[4,4,64,640]{3,2,1,0:T(8,128)}, u32[]{:S(2)}, u32[]{:S(2)}) %all-to-all-start.6) | async-done | bytes 2621472 | tf_op jit(solution)/shard_map/all_to_all | solution.py:256
  768.8 3.7 all-to-all-start.7
  787.3 16.5 %all-to-all-done.7 = f32[4,4,64,640]{3,2,1,0:T(8,128)S(1)} async-done(((f32[4,4,64,640]{3,2,1,0:T(8,128)}), f32[4,4,64,640]{3,2,1,0:T(8,128)S(1)}, u32[]{:S(2)}, u32[]{:S(2)}) %all-to-all-start.7) | async-done | bytes 2621472 | tf_op jit(solution)/shard_map/all_to_all | solution.py:256
  805.6 25.7 %shard_map.65 = f32[4,512,2,512]{3,2,1,0:T(2,128)} custom-call(s32[1]{0:T(128)} %bitcast.occ_pos_ref, s32[2,512]{1,0:T(2,128)} %constant_dynamic-slice_fusion.5.key_c_ref, s32[4,512,1]{2,1,0:T(8,128)} %copy.228.slot_r_ref, s32[4]{0:T(128)S(1)} %slice.137.irrep_i_ref, s32[512,1]{1,0:T(8,128)S(1)} %copy-done.27, s32[512,1]{1,0:T(8,128)S(1)} %copy-done.21, ...), custom_call_target="tpu_custom_call" | custom-call | flops 10737418240 | bytes 13631488 | tf_op jit(solution)/shard_map/pallas_call | solution.py:223
  (225 shorter events, 89.7 us)
Async XLA Ops:
  6.5 503.9 %reduce-scatter.11.cloned.1.call-start = ((), (), s32[]{:S(2)}) async-start(), calls=%async_computation.17 | async-start | bytes 3276800 | tf_op jit(solution)/shard_map/reduce_scatter | solution.py:370
  55.2 59.0 %collective-permute-start.25 = (f32[2,2,2,64,1024]{4,3,2,1,0:T(8,128)}, f32[2,2,2,64,1024]{4,3,2,1,0:T(8,128)}, u32[]{:S(2)}, u32[]{:S(2)}) collective-permute-start(f32[2,2,2,64,1024]{4,3,2,1,0:T(8,128)} %get-tuple-element.1196), channel_id=1, source_target_pairs={{0,2},{2,0},{4,6},{6,4},{1,3},{3,1},{5,7},{7,5},{8,10},{10,8},{12,... | collective-permute-start | bytes 6291464 | tf_op jit(solution)/shard_map/ppermute | solution.py:248
  55.7 58.5 %collective-permute-start.26 = (f32[2,2,2,64,1024]{4,3,2,1,0:T(8,128)}, f32[2,2,2,64,1024]{4,3,2,1,0:T(8,128)}, u32[]{:S(2)}, u32[]{:S(2)}) collective-permute-start(f32[2,2,2,64,1024]{4,3,2,1,0:T(8,128)} %get-tuple-element.1195), channel_id=1, source_target_pairs={{0,4},{2,6},{4,0},{6,2},{1,5},{3,7},{5,1},{7,3},{8,12},{10,14},{12... | collective-permute-start | bytes 6291464 | tf_op jit(solution)/shard_map/ppermute | solution.py:248
  58.2 91.4 %collective-permute-start.27 = (f32[2,2,2,64,1024]{4,3,2,1,0:T(8,128)}, f32[2,2,2,64,1024]{4,3,2,1,0:T(8,128)}, u32[]{:S(2)}, u32[]{:S(2)}) collective-permute-start(f32[2,2,2,64,1024]{4,3,2,1,0:T(8,128)} %get-tuple-element.1194), channel_id=1, source_target_pairs={{0,6},{2,4},{4,2},{6,0},{1,7},{3,5},{5,3},{7,1},{8,14},{10,12},{12... | collective-permute-start | bytes 6291464 | tf_op jit(solution)/shard_map/ppermute | solution.py:248
  152.8 42.2 %copy-start = (f32[4,2,2,2,64,1024]{5,4,3,2,1,0:T(8,128)}, f32[4,2,2,2,64,1024]{5,4,3,2,1,0:T(8,128)S(1)}, u32[]{:S(2)}) copy-start(f32[4,2,2,2,64,1024]{5,4,3,2,1,0:T(8,128)S(1)} %pad_maximum_fusion.7) | copy-start | bytes 25165828
  153.3 24.7 %collective-permute-start.28 = (f32[2,64,1024]{2,1,0:T(8,128)S(1)}, f32[2,64,1024]{2,1,0:T(8,128)S(1)}, u32[]{:S(2)}, u32[]{:S(2)}) collective-permute-start(f32[2,64,1024]{2,1,0:T(8,128)S(1)} %get-tuple-element.1212), channel_id=1, source_target_pairs={{0,8},{8,0},{16,24},{24,16},{1,9},{9,1},{17,25},{25,17},{2,10},{10... | collective-permute-start | bytes 1572872 | tf_op jit(solution)/shard_map/ppermute | solution.py:248
  154.9 38.2 %collective-permute-start.29 = (f32[2,64,1024]{2,1,0:T(8,128)S(1)}, f32[2,64,1024]{2,1,0:T(8,128)S(1)}, u32[]{:S(2)}, u32[]{:S(2)}) collective-permute-start(f32[2,64,1024]{2,1,0:T(8,128)S(1)} %get-tuple-element.1211), channel_id=1, source_target_pairs={{0,16},{8,24},{16,0},{24,8},{1,17},{9,25},{17,1},{25,9},{2,18},{10... | collective-permute-start | bytes 1572872 | tf_op jit(solution)/shard_map/ppermute | solution.py:248
  157.5 35.6 %collective-permute-start.30 = (f32[2,64,1024]{2,1,0:T(8,128)S(1)}, f32[2,64,1024]{2,1,0:T(8,128)S(1)}, u32[]{:S(2)}, u32[]{:S(2)}) collective-permute-start(f32[2,64,1024]{2,1,0:T(8,128)S(1)} %get-tuple-element.1210), channel_id=1, source_target_pairs={{0,24},{8,16},{16,8},{24,0},{1,25},{9,17},{17,9},{25,1},{2,26},{10... | collective-permute-start | bytes 1572872 | tf_op jit(solution)/shard_map/ppermute | solution.py:248
  193.3 51.4 %collective-permute-start.34 = (f32[1,4,2,64,1024]{4,3,2,1,0:T(8,128)S(1)}, f32[1,4,2,64,1024]{4,3,2,1,0:T(8,128)S(1)}, u32[]{:S(2)}, u32[]{:S(2)}) collective-permute-start(f32[1,4,2,64,1024]{4,3,2,1,0:T(8,128)S(1)} %maximum_bitcast_fusion.4), channel_id=1, source_target_pairs={{0,4},{2,6},{4,0},{6,2},{1,5},{3,7},{5,1},{7,3},{8,12},{10,14},{12... | collective-permute-start | bytes 6291464 | tf_op jit(solution)/shard_map/ppermute | solution.py:248
  195.4 31.7 %collective-permute-start.31 = (f32[2,64,1024]{2,1,0:T(8,128)S(1)}, f32[2,64,1024]{2,1,0:T(8,128)S(1)}, u32[]{:S(2)}, u32[]{:S(2)}) collective-permute-start(f32[2,64,1024]{2,1,0:T(8,128)S(1)} %get-tuple-element.1208), channel_id=1, source_target_pairs={{0,8},{8,0},{16,24},{24,16},{1,9},{9,1},{17,25},{25,17},{2,10},{10... | collective-permute-start | bytes 1572872 | tf_op jit(solution)/shard_map/ppermute | solution.py:248
  206.3 38.2 %collective-permute-start.32 = (f32[2,64,1024]{2,1,0:T(8,128)S(1)}, f32[2,64,1024]{2,1,0:T(8,128)S(1)}, u32[]{:S(2)}, u32[]{:S(2)}) collective-permute-start(f32[2,64,1024]{2,1,0:T(8,128)S(1)} %get-tuple-element.1207), channel_id=1, source_target_pairs={{0,16},{8,24},{16,0},{24,8},{1,17},{9,25},{17,1},{25,9},{2,18},{10... | collective-permute-start | bytes 1572872 | tf_op jit(solution)/shard_map/ppermute | solution.py:248
  207.4 37.1 %collective-permute-start.33 = (f32[2,64,1024]{2,1,0:T(8,128)S(1)}, f32[2,64,1024]{2,1,0:T(8,128)S(1)}, u32[]{:S(2)}, u32[]{:S(2)}) collective-permute-start(f32[2,64,1024]{2,1,0:T(8,128)S(1)} %get-tuple-element.1206), channel_id=1, source_target_pairs={{0,24},{8,16},{16,8},{24,0},{1,25},{9,17},{17,9},{25,1},{2,26},{10... | collective-permute-start | bytes 1572872 | tf_op jit(solution)/shard_map/ppermute | solution.py:248
  247.1 7.5 collective-permute-start.39
  271.9 59.2 %collective-permute-start.40 = (f32[4,4,64,640]{3,2,1,0:T(8,128)}, f32[4,4,64,640]{3,2,1,0:T(8,128)}, u32[]{:S(2)}, u32[]{:S(2)}) collective-permute-start(f32[4,4,64,640]{3,2,1,0:T(8,128)} %shard_map.57), channel_id=1, source_target_pairs={{0,1},{1,0},{2,3},{3,2},{4,5},{5,4},{6,7},{7,6},{8,9},{9,8},{10,11... | collective-permute-start | bytes 7864328 | tf_op jit(solution)/shard_map/ppermute | solution.py:359
  273.5 51.6 %collective-permute-start.38 = (f32[1,4,2,64,1024]{4,3,2,1,0:T(8,128)S(1)}, f32[1,4,2,64,1024]{4,3,2,1,0:T(8,128)S(1)}, u32[]{:S(2)}, u32[]{:S(2)}) collective-permute-start(f32[1,4,2,64,1024]{4,3,2,1,0:T(8,128)S(1)} %maximum_bitcast_fusion.5), channel_id=1, source_target_pairs={{0,4},{2,6},{4,0},{6,2},{1,5},{3,7},{5,1},{7,3},{8,12},{10,14},{12... | collective-permute-start | bytes 6291464 | tf_op jit(solution)/shard_map/ppermute | solution.py:248
  276.0 31.4 %collective-permute-start.35 = (f32[2,64,1024]{2,1,0:T(8,128)S(1)}, f32[2,64,1024]{2,1,0:T(8,128)S(1)}, u32[]{:S(2)}, u32[]{:S(2)}) collective-permute-start(f32[2,64,1024]{2,1,0:T(8,128)S(1)} %get-tuple-element.1204), channel_id=1, source_target_pairs={{0,8},{8,0},{16,24},{24,16},{1,9},{9,1},{17,25},{25,17},{2,10},{10... | collective-permute-start | bytes 1572872 | tf_op jit(solution)/shard_map/ppermute | solution.py:248
  285.4 38.2 %collective-permute-start.36 = (f32[2,64,1024]{2,1,0:T(8,128)S(1)}, f32[2,64,1024]{2,1,0:T(8,128)S(1)}, u32[]{:S(2)}, u32[]{:S(2)}) collective-permute-start(f32[2,64,1024]{2,1,0:T(8,128)S(1)} %get-tuple-element.1203), channel_id=1, source_target_pairs={{0,16},{8,24},{16,0},{24,8},{1,17},{9,25},{17,1},{25,9},{2,18},{10... | collective-permute-start | bytes 1572872 | tf_op jit(solution)/shard_map/ppermute | solution.py:248
  286.5 37.1 %collective-permute-start.37 = (f32[2,64,1024]{2,1,0:T(8,128)S(1)}, f32[2,64,1024]{2,1,0:T(8,128)S(1)}, u32[]{:S(2)}, u32[]{:S(2)}) collective-permute-start(f32[2,64,1024]{2,1,0:T(8,128)S(1)} %get-tuple-element.1202), channel_id=1, source_target_pairs={{0,24},{8,16},{16,8},{24,0},{1,25},{9,17},{17,9},{25,1},{2,26},{10... | collective-permute-start | bytes 1572872 | tf_op jit(solution)/shard_map/ppermute | solution.py:248
  331.1 7.5 collective-permute-start.45
  333.0 76.0 %collective-permute-start.44 = (f32[1,4,2,64,1024]{4,3,2,1,0:T(8,128)}, f32[1,4,2,64,1024]{4,3,2,1,0:T(8,128)}, u32[]{:S(2)}, u32[]{:S(2)}) collective-permute-start(f32[1,4,2,64,1024]{4,3,2,1,0:T(8,128)} %maximum_bitcast_fusion.6), channel_id=1, source_target_pairs={{0,4},{2,6},{4,0},{6,2},{1,5},{3,7},{5,1},{7,3},{8,12},{10,14},{12... | collective-permute-start | bytes 6291464 | tf_op jit(solution)/shard_map/ppermute | solution.py:248
  356.5 75.5 %collective-permute-start.46 = (f32[4,4,64,640]{3,2,1,0:T(8,128)}, f32[4,4,64,640]{3,2,1,0:T(8,128)}, u32[]{:S(2)}, u32[]{:S(2)}) collective-permute-start(f32[4,4,64,640]{3,2,1,0:T(8,128)} %shard_map.58), channel_id=1, source_target_pairs={{0,1},{1,0},{2,3},{3,2},{4,5},{5,4},{6,7},{7,6},{8,9},{9,8},{10,11... | collective-permute-start | bytes 7864328 | tf_op jit(solution)/shard_map/ppermute | solution.py:359
  359.4 55.1 %copy-start.48 = (s32[20]{0:T(128)}, s32[20]{0:T(128)S(1)}, u32[]{:S(2)}) copy-start(s32[20]{0:T(128)S(1)} %concatenate.123.scalar_ref) | copy-start | bytes 244
  361.2 31.8 %collective-permute-start.41 = (f32[2,64,1024]{2,1,0:T(8,128)S(1)}, f32[2,64,1024]{2,1,0:T(8,128)S(1)}, u32[]{:S(2)}, u32[]{:S(2)}) collective-permute-start(f32[2,64,1024]{2,1,0:T(8,128)S(1)} %get-tuple-element.1200), channel_id=1, source_target_pairs={{0,8},{8,0},{16,24},{24,16},{1,9},{9,1},{17,25},{25,17},{2,10},{10... | collective-permute-start | bytes 1572872 | tf_op jit(solution)/shard_map/ppermute | solution.py:248
  370.7 38.2 %collective-permute-start.42 = (f32[2,64,1024]{2,1,0:T(8,128)S(1)}, f32[2,64,1024]{2,1,0:T(8,128)S(1)}, u32[]{:S(2)}, u32[]{:S(2)}) collective-permute-start(f32[2,64,1024]{2,1,0:T(8,128)S(1)} %get-tuple-element.1199), channel_id=1, source_target_pairs={{0,16},{8,24},{16,0},{24,8},{1,17},{9,25},{17,1},{25,9},{2,18},{10... | collective-permute-start | bytes 1572872 | tf_op jit(solution)/shard_map/ppermute | solution.py:248
  371.8 37.1 %collective-permute-start.43 = (f32[2,64,1024]{2,1,0:T(8,128)S(1)}, f32[2,64,1024]{2,1,0:T(8,128)S(1)}, u32[]{:S(2)}, u32[]{:S(2)}) collective-permute-start(f32[2,64,1024]{2,1,0:T(8,128)S(1)} %get-tuple-element.1198), channel_id=1, source_target_pairs={{0,24},{8,16},{16,8},{24,0},{1,25},{9,17},{17,9},{25,1},{2,26},{10... | collective-permute-start | bytes 1572872 | tf_op jit(solution)/shard_map/ppermute | solution.py:248
  435.6 113.6 %reduce-scatter.9.cloned.1.call-start = ((), (), s32[]{:S(2)}) async-start(), calls=%async_computation.16 | async-start | bytes 3276800 | tf_op jit(solution)/shard_map/reduce_scatter | solution.py:370
  435.6 7.6 collective-permute-start.48
  440.1 165.6 %reduce-scatter.13.cloned.1.call-start = ((), (), s32[]{:S(2)}) async-start(), calls=%async_computation.18 | async-start | bytes 3276800 | tf_op jit(solution)/shard_map/reduce_scatter | solution.py:370
  440.9 48.1 %collective-permute-start.47 = (f32[1,4,2,64,1024]{4,3,2,1,0:T(8,128)S(1)}, f32[1,4,2,64,1024]{4,3,2,1,0:T(8,128)}, u32[]{:S(2)}, u32[]{:S(2)}) collective-permute-start(f32[1,4,2,64,1024]{4,3,2,1,0:T(8,128)S(1)} %maximum_bitcast_fusion.7), channel_id=1, source_target_pairs={{0,4},{2,6},{4,0},{6,2},{1,5},{3,7},{5,1},{7,3},{8,12},{10,14},{12... | collective-permute-start | bytes 6291464 | tf_op jit(solution)/shard_map/ppermute | solution.py:248
  460.6 88.5 %collective-permute-start.49 = (f32[4,4,64,640]{3,2,1,0:T(8,128)}, f32[4,4,64,640]{3,2,1,0:T(8,128)}, u32[]{:S(2)}, u32[]{:S(2)}) collective-permute-start(f32[4,4,64,640]{3,2,1,0:T(8,128)} %shard_map.61), channel_id=1, source_target_pairs={{0,1},{1,0},{2,3},{3,2},{4,5},{5,4},{6,7},{7,6},{8,9},{9,8},{10,11... | collective-permute-start | bytes 7864328 | tf_op jit(solution)/shard_map/ppermute | solution.py:359
  461.9 31.1 %copy-start.52 = (s32[20]{0:T(128)}, s32[20]{0:T(128)S(1)}, u32[]{:S(2)}) copy-start(s32[20]{0:T(128)S(1)} %concatenate.127.scalar_ref) | copy-start | bytes 244
  549.2 7.5 collective-permute-start.50
  553.5 135.8 %reduce-scatter.15.cloned.1.call-start = ((), (), s32[]{:S(2)}) async-start(), calls=%async_computation.19 | async-start | bytes 3276800 | tf_op jit(solution)/shard_map/reduce_scatter | solution.py:370
  574.7 59.1 %collective-permute-start.51 = (f32[4,4,64,640]{3,2,1,0:T(8,128)}, f32[4,4,64,640]{3,2,1,0:T(8,128)S(1)}, u32[]{:S(2)}, u32[]{:S(2)}) collective-permute-start(f32[4,4,64,640]{3,2,1,0:T(8,128)} %shard_map.63), channel_id=1, source_target_pairs={{0,1},{1,0},{2,3},{3,2},{4,5},{5,4},{6,7},{7,6},{8,9},{9,8},{10,11... | collective-permute-start | bytes 7864328 | tf_op jit(solution)/shard_map/ppermute | solution.py:359
  704.7 64.1 %all-to-all-start.6 = ((f32[4,4,64,640]{3,2,1,0:T(8,128)}), f32[4,4,64,640]{3,2,1,0:T(8,128)}, u32[]{:S(2)}, u32[]{:S(2)}) async-start(f32[4,4,64,640]{3,2,1,0:T(8,128)} %pad_maximum_fusion.13), calls=%async_computation.14 | async-start | bytes 5242880 | tf_op jit(solution)/shard_map/all_to_all | solution.py:256
  711.1 61.5 %copy-start.32 = (s32[4,4]{1,0:T(4,128)S(1)}, s32[4,4]{1,0:T(4,128)}, u32[]{:S(2)}) copy-start(s32[4,4]{1,0:T(4,128)} %copy-done.31) | copy-start | bytes 196
  711.1 67.7 %copy-start.35 = (s32[512]{0:T(512)S(1)}, s32[512]{0:T(512)}, u32[]{:S(2)}) copy-start(s32[512]{0:T(512)} %copy-done.34) | copy-start | bytes 6148
  711.1 67.7 %copy-start.38 = (s32[1,512]{1,0:T(1,128)S(1)}, s32[1,512]{1,0:T(1,128)}, u32[]{:S(2)}) copy-start(s32[1,512]{1,0:T(1,128)} %get-tuple-element.1228) | copy-start | bytes 6148
  711.1 67.7 %copy-start.39 = (s32[1,512]{1,0:T(1,128)S(1)}, s32[1,512]{1,0:T(1,128)}, u32[]{:S(2)}) copy-start(s32[1,512]{1,0:T(1,128)} %get-tuple-element.1229) | copy-start | bytes 6148
  711.1 67.7 %copy-start.40 = (s32[1,512]{1,0:T(1,128)S(1)}, s32[1,512]{1,0:T(1,128)}, u32[]{:S(2)}) copy-start(s32[1,512]{1,0:T(1,128)} %get-tuple-element.1230) | copy-start | bytes 6148
  711.1 69.1 %copy-start.37 = (s32[1,512]{1,0:T(1,128)S(1)}, s32[1,512]{1,0:T(1,128)}, u32[]{:S(2)}) copy-start(s32[1,512]{1,0:T(1,128)} %get-tuple-element.1172) | copy-start | bytes 6148
  711.1 69.5 %copy-start.36 = (s32[512,1]{0,1:T(1,128)S(1)}, s32[512,1]{0,1:T(1,128)}, u32[]{:S(2)}) copy-start(s32[512,1]{0,1:T(1,128)} %get-tuple-element.1173) | copy-start | bytes 6148
  711.1 94.4 %collective-permute-start.52 = (f32[2,512,640]{2,1,0:T(8,128)}, f32[2,512,640]{2,1,0:T(8,128)}, u32[]{:S(2)}, u32[]{:S(2)}) collective-permute-start(f32[2,512,640]{2,1,0:T(8,128)} %bitcast.96.own_ref), channel_id=1, source_target_pairs={{0,1},{1,0},{2,3},{3,2},{4,5},{5,4},{6,7},{7,6},{8,9},{9,8},{10,11... | collective-permute-start | bytes 7864328 | tf_op jit(solution)/shard_map/ppermute | solution.py:380
  768.8 34.9 %all-to-all-start.7 = ((f32[4,4,64,640]{3,2,1,0:T(8,128)}), f32[4,4,64,640]{3,2,1,0:T(8,128)S(1)}, u32[]{:S(2)}, u32[]{:S(2)}) async-start(f32[4,4,64,640]{3,2,1,0:T(8,128)} %all-to-all-done.6), calls=%async_computation.15 | async-start | bytes 5242880 | tf_op jit(solution)/shard_map/all_to_all | solution.py:256
  805.5 25.8 %copy-start.18 = (s32[4,2,4,64,1]{3,2,0,4,1:T(4,128)S(1)}, s32[4,2,4,64,1]{3,2,0,4,1:T(4,128)}, u32[]{:S(2)}) copy-start(s32[4,2,4,64,1]{3,2,0,4,1:T(4,128)} %copy-done.17) | copy-start | bytes 24580
  805.5 25.8 %copy-start.43 = (s32[20]{0:T(128)S(1)}, s32[20]{0:T(128)}, u32[]{:S(2)}) copy-start(s32[20]{0:T(128)} %copy-done.42) | copy-start | bytes 244
  805.5 25.8 %copy-start.45 = (s32[20]{0:T(128)S(1)}, s32[20]{0:T(128)}, u32[]{:S(2)}) copy-start(s32[20]{0:T(128)} %copy-done.44) | copy-start | bytes 244
  805.5 25.8 %copy-start.47 = (s32[20]{0:T(128)S(1)}, s32[20]{0:T(128)}, u32[]{:S(2)}) copy-start(s32[20]{0:T(128)} %copy-done.46) | copy-start | bytes 244
  (28 other events, 344.6 us)
Sparse Core Ops, SparseCore 0:
  435.7 59.2 reduce-scatter.10
  497.4 51.7 reduce-scatter.8
  553.6 51.9 reduce-scatter.12
  637.5 51.7 reduce-scatter.14
